TPU v7x, 768 devices: a whole 4x8x12 slice. The times are simulated.
768 devices in a mesh: lat: 32 (over y, x), lon: 24 (over z, core).
Axes of the slice: x: 4, y: 8, z: 12, core: 2. Of those that a mesh axis runs over, the one named last changes fastest.
Arguments:
- fields: bfloat16 [768, 3072, 128], P('lat', 'lon'), may hold values from -6 to 6
- req_block: int32 [32, 24, 3, 1280], P('lat', 'lon'), may hold values from 0 to 191
- req_stencil: int32 [32, 24, 3, 4, 1280], P('lat', 'lon'), may hold values from 0 to 15
- req_frac: int32 [32, 24, 3, 2, 1280], P('lat', 'lon'), may hold values from 0 to 15
- req_count: int32 [32, 24, 3], P('lat', 'lon'), may hold values from 597 to 1280, as said below
- legendre: bfloat16 [1536, 768, 768], P(('lon', 'lat')), may hold values from -0.21875 to 0.21875
Outputs:
- spectral: float32 [1536, 768, 128], P(('lon', 'lat'))
Inputs may be any that keep to these rules, and one draw needn't show every extreme that they name: `req_count`: the three counts of a tile sum to 3072; positions j at or beyond a slot's count are unused. In every latitude band some tile receives 1280 points from each of the three tiles whose slots reach it, and every tile fills one slot to 1280.
All inputs are finite; a program needn't handle non-finite values.
Results may differ from a plain program's by a relative error of at most 0.0048.
Values may be sent and summed in bfloat16 or wider, within the bound.
A program may use at most 32 MiB of HBM per device.

v0:
```python
import math

import jax
import jax.numpy as jnp
from jax import lax
from jax.sharding import PartitionSpec as P

KF = 1536
NN = 768
BLK = 16
FRAC = 16
COLS = 3072


def padded(cells, sides, width):
    for axis, dim in sides:
        count = lax.axis_size(axis)
        head = lax.slice_in_dim(cells, 0, width, axis=dim)
        tail = lax.slice_in_dim(cells, cells.shape[dim] - width, cells.shape[dim], axis=dim)
        cells = jnp.concatenate(
            [
                lax.ppermute(tail, axis, [(i, (i + 1) % count) for i in range(count)]),
                cells,
                lax.ppermute(head, axis, [((i + 1) % count, i) for i in range(count)]),
            ],
            axis=dim,
        )
    return cells


def hartley_table(lon_total):
    wave_index = jnp.arange(KF, dtype=jnp.int32)
    lon_index = jnp.arange(lon_total, dtype=jnp.int32)
    phase_index = wave_index[:, None] * lon_index[None, :] % lon_total
    phase_angle = 2.0 * math.pi / lon_total * phase_index.astype(jnp.float32)
    return ((jnp.cos(phase_angle) + jnp.sin(phase_angle)) / math.sqrt(lon_total)).astype(
        jnp.bfloat16
    )


def interpolate(own_tile, packed):
    cell_rows = packed[0][None, :] * BLK + packed[1:5]
    picked = jnp.take(own_tile, cell_rows.reshape(-1), axis=0).astype(jnp.float32)
    picked = picked.reshape(4, cell_rows.shape[1], own_tile.shape[1])
    frac_lat = (packed[5].astype(jnp.float32) + 0.5) / FRAC
    frac_lon = (packed[6].astype(jnp.float32) + 0.5) / FRAC
    weights = jnp.stack(
        [
            (1.0 - frac_lat) * (1.0 - frac_lon),
            frac_lat * (1.0 - frac_lon),
            (1.0 - frac_lat) * frac_lon,
            frac_lat * frac_lon,
        ]
    )
    return jnp.sum(weights[:, :, None] * picked, axis=0).astype(jnp.bfloat16)


def place_columns(values, counts):
    slot_ends = jnp.cumsum(counts)
    starts = slot_ends - counts
    column = jnp.arange(COLS, dtype=jnp.int32)
    slot_index = jnp.sum((slot_ends[None, :] <= column[:, None]).astype(jnp.int32), axis=1)
    onehot = slot_index[:, None] == jnp.arange(3, dtype=jnp.int32)[None, :]
    offset = column - jnp.sum(jnp.where(onehot, starts[None, :], 0), axis=1)
    flat_index = slot_index * values.shape[1] + offset
    return jnp.take(values.reshape(-1, values.shape[-1]), flat_index, axis=0)


def local(fields, req_block, req_stencil, req_frac, req_count, legendre):
    lat_rows, lon_cols, channels = fields.shape
    packed = jnp.concatenate(
        [req_block[0, 0][:, None, :], req_stencil[0, 0], req_frac[0, 0]], axis=1
    )
    counts = req_count[0, 0]
    widened = padded(fields, (("lon", 1),), lon_cols)
    slot_values = []
    for slot_index in range(3):
        owner_tile = widened[:, slot_index * lon_cols : (slot_index + 1) * lon_cols, :].reshape(
            -1, channels
        )
        slot_values.append(interpolate(owner_tile, packed[slot_index]))
    departed = place_columns(jnp.stack(slot_values), counts).reshape(lat_rows, lon_cols, channels)
    lon_total = lon_cols * lax.axis_size("lon")
    hartley = hartley_table(lon_total)
    spectra = jnp.einsum(
        "kx,yxc->ykc",
        hartley,
        lax.all_to_all(departed, "lon", split_axis=0, concat_axis=1, tiled=True),
        preferred_element_type=jnp.float32,
    )
    fourier = lax.all_to_all(
        spectra.astype(jnp.bfloat16), "lon", split_axis=1, concat_axis=0, tiled=True
    )
    gathered = lax.all_to_all(fourier, "lat", split_axis=1, concat_axis=0, tiled=True)
    projected = jnp.einsum("kyn,ykc->knc", legendre, gathered, preferred_element_type=jnp.float32)
    degree = jnp.arange(legendre.shape[2], dtype=jnp.float32)
    factor = 1.0 / (1.0 + 4.0 * degree * (degree + 1.0) / (NN * (NN + 1)))
    return projected * factor[None, :, None]


def solution(mesh):
    return jax.shard_map(
        local,
        mesh=mesh,
        in_specs=(
            P("lat", "lon", None),
            P("lat", "lon", None, None),
            P("lat", "lon", None, None, None),
            P("lat", "lon", None, None, None),
            P("lat", "lon", None),
            P(("lon", "lat"), None, None),
        ),
        out_specs=P(("lon", "lat"), None, None),
        check_vma=False,
    )
```

profile of v0, /device:TPU:1, one launch (start us, length us, event | category | flops | bytes accessed | tf_op | source)
XLA Modules:
  0.0 277.4 jit_solution(4827348516803703569)
XLA Ops:
  0.0 0.0 copy-start
  0.0 0.0 copy-start.1
  0.0 3.5 %collective-permute-start = (bf16[24,128,128]{2,1,0:T(8,128)(2,1)}, bf16[24,128,128]{2,1,0:T(8,128)(2,1)}, u32[]{:S(2)}, u32[]{:S(2)}) collective-permute-start(bf16[24,128,128]{2,1,0:T(8,128)(2,1)} %param.8), channel_id=1, source_target_pairs={{0,1},{1,2},{2,3},{3,4},{4,5},{5,6},{6,7},{7,8},{8,9},{9,10},{10,1... | collective-permute-start | bytes 2359304 | tf_op jit(solution)/shard_map/ppermute | solution.py:22
  3.5 7.0 %collective-permute-start.1 = (bf16[24,128,128]{2,1,0:T(8,128)(2,1)}, bf16[24,128,128]{2,1,0:T(8,128)(2,1)}, u32[]{:S(2)}, u32[]{:S(2)}) collective-permute-start(bf16[24,128,128]{2,1,0:T(8,128)(2,1)} %param.8), channel_id=1, source_target_pairs={{1,0},{2,1},{3,2},{4,3},{5,4},{6,5},{7,6},{8,7},{9,8},{10,9},{11,1... | collective-permute-start | bytes 2359304 | tf_op jit(solution)/shard_map/ppermute | solution.py:24
  10.5 0.8 subtract_multiply_fusion.6
  11.3 0.8 subtract_multiply_fusion.7
  12.1 0.8 multiply_reduce_fusion.2
  13.0 0.8 fusion.42
  13.8 0.8 reduce-window.7
  14.6 0.7 bitcast_subtract_fusion.1
  15.3 0.1 convert_reduce_fusion
  15.4 0.1 select_reduce_fusion
  15.7 0.0 copy-done.1
  15.7 18.6 %gather_fusion.2 = bf16[5120,128]{1,0:T(8,128)(2,1)} fusion(bf16[3072,128]{1,0:T(8,128)(2,1)S(1)} %bitcast.120, s32[5120]{0:T(1024)S(1)} %broadcast_clamp_fusion.1), kind=kCustom, calls=%fused_computation.1.clone | custom fusion | bytes 2641920 | tf_op jit(solution)/shard_map/jit(_take)/gather | solution.py:43
  34.3 3.7 %broadcast_select_fusion.1 = bf16[5120,128]{1,0:T(8,128)(2,1)S(1)} fusion(bf16[5120,128]{1,0:T(8,128)(2,1)} %gather_fusion.2, pred[5120]{0:T(1024)(128)(4,1)S(1)} %compare_and_fusion.1), kind=kLoop, calls=%fused_computation.22 | loop fusion | flops 655360 | bytes 2626560 | tf_op jit(solution)/shard_map/jit(_take)/select_n | solution.py:43
  38.1 1.6 fusion.7
  39.8 0.0 collective-permute-done
  39.8 19.1 %gather_fusion.1 = bf16[5120,128]{1,0:T(8,128)(2,1)} fusion(bf16[3072,128]{1,0:T(8,128)(2,1)} %bitcast.8, s32[5120]{0:T(1024)S(1)} %broadcast_clamp_fusion.2), kind=kCustom, calls=%fused_computation.clone | custom fusion | bytes 2641920 | tf_op jit(solution)/shard_map/jit(_take)/gather | solution.py:43
  58.9 3.7 %broadcast_select_fusion.2 = bf16[5120,128]{1,0:T(8,128)(2,1)S(1)} fusion(bf16[5120,128]{1,0:T(8,128)(2,1)} %gather_fusion.1, pred[5120]{0:T(1024)(128)(4,1)S(1)} %compare_and_fusion.2), kind=kLoop, calls=%fused_computation.23 | loop fusion | flops 655360 | bytes 2626560 | tf_op jit(solution)/shard_map/jit(_take)/select_n | solution.py:43
  62.6 1.7 fusion.8
  64.3 0.0 collective-permute-done.1
  64.3 19.1 %gather_fusion.3 = bf16[5120,128]{1,0:T(8,128)(2,1)} fusion(bf16[3072,128]{1,0:T(8,128)(2,1)} %bitcast.18, s32[5120]{0:T(1024)S(1)} %broadcast_clamp_fusion), kind=kCustom, calls=%fused_computation.2.clone | custom fusion | bytes 2641920 | tf_op jit(solution)/shard_map/jit(_take)/gather | solution.py:43
  83.4 0.0 copy-start.2
  83.4 0.0 copy-start.3
  83.4 3.8 %broadcast_select_fusion = bf16[5120,128]{1,0:T(8,128)(2,1)S(1)} fusion(bf16[5120,128]{1,0:T(8,128)(2,1)} %gather_fusion.3, pred[5120]{0:T(1024)(128)(4,1)S(1)} %compare_and_fusion), kind=kLoop, calls=%fused_computation.21 | loop fusion | flops 655360 | bytes 2626560 | tf_op jit(solution)/shard_map/jit(_take)/select_n | solution.py:43
  87.2 0.9 fusion.6
  88.1 0.0 copy-done.2
  88.1 0.0 copy-done.3
  88.1 0.1 pad_maximum_fusion
  88.2 11.5 %gather_fusion = bf16[3072,128]{1,0:T(8,128)(2,1)} fusion(bf16[3840,128]{1,0:T(8,128)(2,1)S(1)} %bitcast.121, s32[3072]{0:T(1024)S(1)} %broadcast_clamp_fusion.3), kind=kCustom, calls=%fused_computation.3 | custom fusion | bytes 1585152 | tf_op jit(solution)/shard_map/jit(_take)/gather | solution.py:66
  99.8 1.6 broadcast_select_fusion.3
  101.4 38.6 %all_to_all.39 = bf16[24,128,128]{2,1,0:T(8,128)(2,1)S(1)} all-to-all(bf16[24,128,128]{2,1,0:T(8,128)(2,1)S(1)} %broadcast_select_fusion.3), channel_id=1, replica_groups=mesh['lat'=32,'lon'=24] {'lon'}, dimensions={0} | all-to-all | bytes 1572864 | tf_op jit(solution)/shard_map/all_to_all | solution.py:88
  139.9 79.2 %fusion.10 = bf16[1,1536,128]{1,2,0:T(8,128)(2,1)S(1)} fusion(bf16[3072,128]{1,0:T(8,128)(2,1)S(1)} %bitcast.134), kind=kOutput, calls=%fused_computation.20 | convolution fusion | flops 1264779264 | bytes 1179648 | tf_op jit(solution)/shard_map/kx,yxc->ykc/dot_general | solution.py:85
  219.1 0.6 copy.19
  219.7 0.5 broadcast.575
  220.2 8.8 %reduce.6 = bf16[1536,128]{1,0:T(8,128)(2,1)S(1)} reduce(bf16[1536,1,128]{2,1,0:T(2,128)(2,1)S(1)} %bitcast.125, bf16[]{:T(256)} %broadcast.575), dimensions={1}, to_apply=%bitcast.113.reduce_sub_computation | reduce | bytes 786434
  229.1 0.1 reshape.544
  229.1 23.9 %all_to_all.40 = bf16[24,2,4096]{2,1,0:T(2,128)(2,1)S(1)} all-to-all(bf16[24,2,4096]{2,1,0:T(2,128)(2,1)S(1)} %reshape.544), channel_id=1, replica_groups=mesh['lat'=32,'lon'=24] {'lon'}, dimensions={0} | all-to-all | bytes 786432 | tf_op jit(solution)/shard_map/all_to_all | solution.py:91
  253.0 0.4 reshape.545
  253.4 0.1 copy.25
  253.5 1.0 copy.20
  254.5 9.7 %all-to-all-start.2 = ((bf16[24,64,128]{2,0,1:T(8,128)(2,1)}), bf16[24,64,128]{2,0,1:T(8,128)(2,1)S(1)}, u32[]{:S(2)}, u32[]{:S(2)}) async-start(bf16[24,64,128]{2,0,1:T(8,128)(2,1)} %copy.20), calls=%async_computation.2 | async-start | bytes 786432 | tf_op jit(solution)/shard_map/all_to_all | solution.py:94
  264.2 11.5 %all-to-all-done.2 = bf16[24,64,128]{2,0,1:T(8,128)(2,1)S(1)} async-done(((bf16[24,64,128]{2,0,1:T(8,128)(2,1)}), bf16[24,64,128]{2,0,1:T(8,128)(2,1)S(1)}, u32[]{:S(2)}, u32[]{:S(2)}) %all-to-all-start.2) | async-done | bytes 393248 | tf_op jit(solution)/shard_map/all_to_all | solution.py:94
  275.7 0.0 copy-done
  275.7 0.5 fusion.11
  276.2 1.1 copy.23
  (23 shorter events, 0.3 us)
Async XLA Ops:
  0.0 275.7 %copy-start = (bf16[2,768,768]{2,1,0:T(8,128)(2,1)S(1)}, bf16[2,768,768]{2,1,0:T(8,128)(2,1)}, u32[]{:S(2)}) copy-start(bf16[2,768,768]{2,1,0:T(8,128)(2,1)} %param.13) | copy-start | bytes 7077892
  0.0 15.7 %copy-start.1 = (bf16[24,128,128]{2,1,0:T(8,128)(2,1)S(1)}, bf16[24,128,128]{2,1,0:T(8,128)(2,1)}, u32[]{:S(2)}) copy-start(bf16[24,128,128]{2,1,0:T(8,128)(2,1)} %param.8) | copy-start | bytes 2359300
  0.0 39.8 %collective-permute-start = (bf16[24,128,128]{2,1,0:T(8,128)(2,1)}, bf16[24,128,128]{2,1,0:T(8,128)(2,1)}, u32[]{:S(2)}, u32[]{:S(2)}) collective-permute-start(bf16[24,128,128]{2,1,0:T(8,128)(2,1)} %param.8), channel_id=1, source_target_pairs={{0,1},{1,2},{2,3},{3,4},{4,5},{5,6},{6,7},{7,8},{8,9},{9,10},{10,1... | collective-permute-start | bytes 2359304 | tf_op jit(solution)/shard_map/ppermute | solution.py:22
  3.5 60.8 %collective-permute-start.1 = (bf16[24,128,128]{2,1,0:T(8,128)(2,1)}, bf16[24,128,128]{2,1,0:T(8,128)(2,1)}, u32[]{:S(2)}, u32[]{:S(2)}) collective-permute-start(bf16[24,128,128]{2,1,0:T(8,128)(2,1)} %param.8), channel_id=1, source_target_pairs={{1,0},{2,1},{3,2},{4,3},{5,4},{6,5},{7,6},{8,7},{9,8},{10,9},{11,1... | collective-permute-start | bytes 2359304 | tf_op jit(solution)/shard_map/ppermute | solution.py:24
  83.4 4.7 %copy-start.2 = (bf16[1280,128]{1,0:T(8,128)(2,1)S(1)}, bf16[1280,128]{1,0:T(8,128)(2,1)}, u32[]{:S(2)}) copy-start(bf16[1280,128]{1,0:T(8,128)(2,1)} %fusion.7) | copy-start | bytes 983044
  83.4 4.7 %copy-start.3 = (bf16[1280,128]{1,0:T(8,128)(2,1)S(1)}, bf16[1280,128]{1,0:T(8,128)(2,1)}, u32[]{:S(2)}) copy-start(bf16[1280,128]{1,0:T(8,128)(2,1)} %fusion.8) | copy-start | bytes 983044
  254.5 21.2 %all-to-all-start.2 = ((bf16[24,64,128]{2,0,1:T(8,128)(2,1)}), bf16[24,64,128]{2,0,1:T(8,128)(2,1)S(1)}, u32[]{:S(2)}, u32[]{:S(2)}) async-start(bf16[24,64,128]{2,0,1:T(8,128)(2,1)} %copy.20), calls=%async_computation.2 | async-start | bytes 786432 | tf_op jit(solution)/shard_map/all_to_all | solution.py:94
where the time goes:
time: 281 us; the launch traced here: 277 us
  matrix products  79.7 us (28%)
  local copies, waits for them, and re-layouts  73 us (26%)
  blocking collectives  62.5 us (22%)
  other arithmetic  30.3 us (11%)
  starting transfers between devices  20.1 us (7%)
  waiting for transfers between devices  11.5 us (4%)
    dot_general x1, matrix products, local(): jnp.einsum('kx,yxc->ykc', hartley, lax.all_to_all(departed, 'lon', split_...  79.2 us
    gather x3, local copies, waits for them, and re-layouts, interpolate(): jnp.take(own_tile, cell_rows.reshape(-1), axis=0).astype(jnp.float32)  56.7 us
    all_to_all x1, blocking collectives, local(): lax.all_to_all(departed, 'lon', split_axis=0, concat_axis=1, tiled=True)  38.6 us
    all_to_all x1, blocking collectives, local(): lax.all_to_all(spectra.astype(jnp.bfloat16), 'lon', split_axis=1, concat_...  23.9 us
    gather x1, local copies, waits for them, and re-layouts, place_columns(): return jnp.take(values.reshape(-1, values.shape[-1]), flat_index, axis=0)  11.5 us
    all_to_all x1, waiting for transfers between devices, local(): lax.all_to_all(fourier, 'lat', split_axis=1, concat_axis=0, tiled=True)  11.5 us
    select_n x3, other arithmetic, interpolate(): jnp.take(own_tile, cell_rows.reshape(-1), axis=0).astype(jnp.float32)  11.3 us
    all_to_all x1, starting transfers between devices, local(): lax.all_to_all(fourier, 'lat', split_axis=1, concat_axis=0, tiled=True)  9.66 us
  transfers between devices with their start and end apart: 3, of which 1 were waited for; matrix products, arithmetic and copies ran while one was open for 19% of the time, Pallas kernels for 0%

commit v1 on v0

v1 whole, which is shorter than its diff:
```python
import functools
import math

import jax
import jax.numpy as jnp
import numpy as np
from jax import lax
from jax.experimental import pallas as pl
from jax.experimental.pallas import tpu as pltpu
from jax.sharding import PartitionSpec as P

KF = 1536
NN = 768
BLK = 16
FRAC = 16
COLS = 3072
CAP = 1280
NLON = 3072
BLOCKS = COLS // BLK
FINE = 48


def small_tables():
    unit = 2.0 * math.pi / NLON
    fine = np.arange(FINE, dtype=np.int64)[:, None]
    lane = np.arange(128, dtype=np.int64)[None, :]
    scale = 1.0 / math.sqrt(NLON)
    near = unit * (fine * lane % NLON)
    plus = (np.cos(near) + np.sin(near)) * scale
    minus = (np.cos(near) - np.sin(near)) * scale
    far = unit * (fine * lane * 128 % NLON)
    coarse = unit * (np.arange(KF // FINE, dtype=np.int64)[:, None] * FINE * lane % NLON)
    tables = [plus, minus, np.cos(far), np.sin(far), np.cos(coarse), np.sin(coarse)]
    return [np.asarray(t, dtype=np.float32) for t in tables]


def cell_requests(req_block, req_stencil, req_frac, counts):
    packed = (
        (req_block << 24)
        | (req_stencil[:, 0] << 20)
        | (req_stencil[:, 1] << 16)
        | (req_stencil[:, 2] << 12)
        | (req_stencil[:, 3] << 8)
        | (req_frac[:, 0] << 4)
        | req_frac[:, 1]
    )
    first = counts[0]
    second = first + counts[1]
    cells = jnp.zeros((COLS + CAP,), jnp.int32)
    cells = lax.dynamic_update_slice(cells, packed[0], (0,))
    cells = lax.dynamic_update_slice(cells, packed[1], (first,))
    cells = lax.dynamic_update_slice(cells, packed[2], (second,))
    return cells[:COLS].reshape(COLS // 128, 128), jnp.stack([first, second])


def decode(ends_ref, cells_ref, onehot_ref, weight_ref):
    rows = cells_ref.shape[0]
    columns = jnp.concatenate(
        [cells_ref[...], jnp.zeros((128 - rows, 128), jnp.int32)], axis=0
    ).T
    lane = lax.broadcasted_iota(jnp.int32, (128, 128), 1)
    sub = lax.broadcasted_iota(jnp.int32, (128, 128), 0)
    for row in range(rows):
        word = jnp.broadcast_to(columns[:, row : row + 1], (128, 128))
        block = lax.shift_right_logical(word, 24)
        edge = ends_ref[0] if row < rows // 2 else ends_ref[1]
        block = block + jnp.where(sub + row * 128 >= edge, BLOCKS, 0)
        here = pl.ds(row * 128, 128)
        for part in range(3):
            onehot_ref[here, part * 128 : (part + 1) * 128] = jnp.where(
                block == lane + part * 128, 1.0, 0.0
            ).astype(jnp.bfloat16)
        frac_lat = ((lax.shift_right_logical(word, 4) & 15).astype(jnp.float32) + 0.5) / FRAC
        frac_lon = ((word & 15).astype(jnp.float32) + 0.5) / FRAC
        corner = (
            (1.0 - frac_lat) * (1.0 - frac_lon),
            frac_lat * (1.0 - frac_lon),
            (1.0 - frac_lat) * frac_lon,
            frac_lat * frac_lon,
        )
        weight = jnp.zeros((128, 128), jnp.float32)
        for k in range(4):
            spot = lax.shift_right_logical(word, 20 - 4 * k) & 15
            weight = weight + jnp.where(spot == lane, corner[k], 0.0)
        weight_ref[here, :] = weight


def interpolate_kernel(ends_ref, cells_ref, left_ref, own_ref, right_ref, out_ref, tiles, onehot, weight):
    tiles[:BLOCKS, :] = left_ref[...]
    tiles[BLOCKS : 2 * BLOCKS, :] = own_ref[...]
    tiles[2 * BLOCKS :, :] = right_ref[...]
    decode(ends_ref, cells_ref, onehot, weight)
    step = 512
    for half in range(2):
        low = half * BLOCKS
        for part in range(COLS // 2 // step):
            here = pl.ds(half * (COLS // 2) + part * step, step)
            total = jnp.zeros((step, 128), jnp.float32)
            for pair in range(BLK // 2):
                got = jnp.dot(
                    onehot[here, :],
                    tiles[low : low + 2 * BLOCKS, pair * 256 : (pair + 1) * 256],
                    preferred_element_type=jnp.float32,
                )
                scale = weight[here, :]
                total = total + scale[:, 2 * pair : 2 * pair + 1] * got[:, :128]
                total = total + scale[:, 2 * pair + 1 : 2 * pair + 2] * got[:, 128:]
            out_ref[here, :] = total.astype(jnp.bfloat16)


def interpolate(ends, cells, left, own, right):
    vmem = pl.BlockSpec(memory_space=pltpu.VMEM)
    return pl.pallas_call(
        interpolate_kernel,
        out_shape=jax.ShapeDtypeStruct((COLS, 128), jnp.bfloat16),
        in_specs=[pl.BlockSpec(memory_space=pltpu.SMEM), vmem, vmem, vmem, vmem],
        out_specs=vmem,
        scratch_shapes=[
            pltpu.VMEM((3 * BLOCKS, BLK * 128), jnp.bfloat16),
            pltpu.VMEM((COLS, 2 * BLOCKS), jnp.bfloat16),
            pltpu.VMEM((COLS, 128), jnp.float32),
        ],
        compiler_params=pltpu.CompilerParams(vmem_limit_bytes=40 << 20),
        name="interpolate",
    )(ends, cells, left, own, right)


def fill_table(small, plus, minus, table):
    near_plus, near_minus, far_cos, far_sin, coarse_cos, coarse_sin = small
    for sector in range(NLON // 128):
        here = pl.ds(sector * 128, 128)
        turn_cos = far_cos[:, sector : sector + 1]
        turn_sin = far_sin[:, sector : sector + 1]
        plus[:, here] = turn_cos * near_plus[...] + turn_sin * near_minus[...]
        minus[:, here] = turn_cos * near_minus[...] - turn_sin * near_plus[...]

    def body(step, carry):
        cos = coarse_cos[pl.ds(step, 1), :]
        sin = coarse_sin[pl.ds(step, 1), :]
        rows = pl.ds(pl.multiple_of(step * FINE, FINE), FINE)
        for sector in range(NLON // 128):
            here = slice(sector * 128, (sector + 1) * 128)
            table[sector // 2, rows, (sector % 2) * 128 : (sector % 2 + 1) * 128] = (
                cos * plus[:, here] + sin * minus[:, here]
            ).astype(jnp.bfloat16)
        return carry

    lax.fori_loop(0, KF // FINE, body, 0)


def hartley_kernel(rows_ref, *refs):
    small, out_ref, plus, minus, table = refs[:6], refs[6], refs[7], refs[8], refs[9]
    fill_table(small, plus, minus, table)
    step = 512
    for part in range(KF // step):
        total = jnp.zeros((step, 128), jnp.float32)
        for pair in range(NLON // 256):
            total = total + jnp.dot(
                table[pair, part * step : (part + 1) * step, :],
                rows_ref[pair * 256 : (pair + 1) * 256, :],
                preferred_element_type=jnp.float32,
            )
        out_ref[part * step : (part + 1) * step, :] = total.astype(jnp.bfloat16)


def hartley(rows):
    vmem = pl.BlockSpec(memory_space=pltpu.VMEM)
    return pl.pallas_call(
        hartley_kernel,
        out_shape=jax.ShapeDtypeStruct((KF, 128), jnp.bfloat16),
        in_specs=[vmem] * 7,
        out_specs=vmem,
        scratch_shapes=[
            pltpu.VMEM((FINE, NLON), jnp.float32),
            pltpu.VMEM((FINE, NLON), jnp.float32),
            pltpu.VMEM((NLON // 256, KF, 256), jnp.bfloat16),
        ],
        compiler_params=pltpu.CompilerParams(vmem_limit_bytes=40 << 20),
        name="hartley",
    )(rows, *small_tables())


def local(fields, req_block, req_stencil, req_frac, req_count, legendre):
    lon = lax.axis_size("lon")
    lat = lax.axis_size("lat")
    tile = fields.reshape(BLOCKS, BLK * 128)
    left = lax.ppermute(tile, "lon", [(i, (i + 1) % lon) for i in range(lon)])
    right = lax.ppermute(tile, "lon", [((i + 1) % lon, i) for i in range(lon)])
    cells, ends = cell_requests(req_block[0, 0], req_stencil[0, 0], req_frac[0, 0], req_count[0, 0])
    departed = interpolate(ends, cells, left, tile, right)
    rows = lax.all_to_all(departed.reshape(24, 128, 128), "lon", split_axis=0, concat_axis=0, tiled=True)
    spectra = hartley(rows.reshape(NLON, 128))
    fourier = lax.all_to_all(
        spectra.reshape(lon, KF // lon, 128), "lon", split_axis=0, concat_axis=0, tiled=True
    )
    gathered = lax.all_to_all(fourier, "lat", split_axis=1, concat_axis=0, tiled=True)
    projected = jnp.einsum("kyn,ykc->knc", legendre, gathered, preferred_element_type=jnp.float32)
    degree = jnp.arange(NN, dtype=jnp.float32)
    factor = 1.0 / (1.0 + 4.0 * degree * (degree + 1.0) / (NN * (NN + 1)))
    return projected * factor[None, :, None]


def solution(mesh):
    return jax.shard_map(
        local,
        mesh=mesh,
        in_specs=(
            P("lat", "lon", None),
            P("lat", "lon", None, None),
            P("lat", "lon", None, None, None),
            P("lat", "lon", None, None, None),
            P("lat", "lon", None),
            P(("lon", "lat"), None, None),
        ),
        out_specs=P(("lon", "lat"), None, None),
        check_vma=False,
    )
```

time: 281 us -> 130 us (0.46)
  the two profiles are of different devices: /device:TPU:1 before, /device:TPU:8 now
where the time goes in v1:
time: 130 us
  blocking collectives  64.3 us (49%)
  starting transfers between devices  22.3 us (17%)
  Pallas kernels  16.4 us (13%)
  waiting for transfers between devices  14.2 us (11%)
  local copies, waits for them, and re-layouts  7.5 us (6%)
  between operations  3.28 us (3%)
  other arithmetic  1.45 us (1%)
    all_to_all x1, blocking collectives, local(): lax.all_to_all(departed.reshape(24, 128, 128), 'lon', split_axis=0, conca...  40.2 us
    all_to_all x1, blocking collectives, local(): lax.all_to_all(spectra.reshape(lon, KF // lon, 128), 'lon', split_axis=0,...  24.1 us
    all_to_all x1, waiting for transfers between devices, local(): lax.all_to_all(fourier, 'lat', split_axis=1, concat_axis=0, tiled=True)  12.8 us
    ppermute x1, starting transfers between devices, local(): right = lax.ppermute(tile, 'lon', [((i + 1) % lon, i) for i in range(lon)])  12.1 us
    pallas_call x1, Pallas kernels, interpolate(): pl.pallas_call(interpolate_kernel, out_shape=jax.ShapeDtypeStruct((COLS,...  10.7 us
    all_to_all x1, starting transfers between devices, local(): lax.all_to_all(fourier, 'lat', split_axis=1, concat_axis=0, tiled=True)  10.2 us
    pallas_call x1, Pallas kernels, hartley(): pl.pallas_call(hartley_kernel, out_shape=jax.ShapeDtypeStruct((KF, 128),...  5.71 us
  transfers between devices with their start and end apart: 3, of which 2 were waited for; matrix products, arithmetic and copies ran while one was open for 4% of the time, Pallas kernels for 0%

profile of v1, /device:TPU:8, one launch (start us, length us, event | category | flops | bytes accessed | tf_op | source)
XLA Modules:
  0.0 130.0 jit_solution(10878268185785489955)
XLA Ops:
  0.0 0.0 copy-start
  0.0 1.6 %reshape.47.own_ref = bf16[192,2048]{1,0:T(8,128)(2,1)S(1)} reshape(bf16[24,128,128]{2,1,0:T(8,128)(2,1)} %param.12) | data formatting | bytes 1572864 | tf_op jit(solution)/shard_map/reshape | solution.py:186
  1.6 0.0 collective-permute-start
  1.6 12.1 %collective-permute-start.1 = (bf16[192,2048]{1,0:T(8,128)(2,1)S(1)}, bf16[192,2048]{1,0:T(8,128)(2,1)}, u32[]{:S(2)}, u32[]{:S(2)}) collective-permute-start(bf16[192,2048]{1,0:T(8,128)(2,1)S(1)} %reshape.47.own_ref), channel_id=1, source_target_pairs={{1,0},{2,1},{3,2},{4,3},{5,4},{6,5},{7,6},{8,7},{9,8},{10,9},{11,1... | collective-permute-start | bytes 2359304 | tf_op jit(solution)/shard_map/ppermute | solution.py:188
  13.7 1.3 %fusion.17 = (s32[1,1,1]{2,1,0:T(1,128)}, s32[1,1,1]{2,1,0:T(1,128)}) fusion(s32[1,1,3]{2,1,0:T(1,128)} %param.16), kind=kLoop, calls=%fused_computation.32 | loop fusion | bytes 16 | tf_op jit(solution)/shard_map/slice | solution.py:48
  17.6 0.9 fusion.16
  18.4 0.9 copy.50
  19.3 0.7 fusion.4
  20.7 0.3 dynamic_update_slice.10
  21.1 0.3 dynamic_update_slice.11
  21.4 0.7 pad_add_fusion.ends_ref
  22.1 0.0 copy-start.1
  22.1 0.0 copy-start.2
  22.1 0.0 copy-start.3
  22.1 0.0 copy-start.4
  22.1 0.0 copy-start.5
  22.1 0.0 copy-start.6
  22.1 1.4 %collective-permute-done.left_ref = bf16[192,2048]{1,0:T(8,128)(2,1)} collective-permute-done((bf16[192,2048]{1,0:T(8,128)(2,1)S(1)}, bf16[192,2048]{1,0:T(8,128)(2,1)}, u32[]{:S(2)}, u32[]{:S(2)}) %collective-permute-start) | collective-permute-done | bytes 786464 | tf_op jit(solution)/shard_map/ppermute | solution.py:187
  23.5 0.0 collective-permute-done.1.right_ref
  23.5 10.7 %interpolate.1 = bf16[3072,128]{1,0:T(8,128)(2,1)S(1)} custom-call(s32[2]{0:T(128)S(1)} %pad_add_fusion.ends_ref, s32[24,128]{1,0:T(8,128)S(1)} %slice_bitcast_fusion.cells_ref, bf16[192,2048]{1,0:T(8,128)(2,1)} %collective-permute-done.left_ref, bf16[192,2048]{1,0:T(8,128)(2,1)S(1)} %reshape.47.own_ref, bf16[192,2048]{1,0:T(8,128)(2,1)} %collective-permute-done.1.right_ref), custom_call_target="tpu_custom_call" | custom-call | tf_op jit(solution)/shard_map/interpolate/pallas_call | solution.py:113
  34.2 40.2 %all_to_all.28 = bf16[24,128,128]{2,1,0:T(8,128)(2,1)S(1)} all-to-all(bf16[24,128,128]{2,1,0:T(8,128)(2,1)S(1)} %bitcast.56), channel_id=1, replica_groups=mesh['lat'=32,'lon'=24] {'lon'}, dimensions={0} | all-to-all | bytes 1572864 | tf_op jit(solution)/shard_map/all_to_all | solution.py:191
  74.4 0.0 copy-done.1
  74.4 0.0 copy-done.2
  74.4 0.0 copy-done.3
  74.4 0.0 copy-done.4
  74.5 0.0 copy-done.5
  74.5 0.0 copy-done.6
  74.5 5.7 %hartley.1 = bf16[1536,128]{1,0:T(8,128)(2,1)S(1)} custom-call(bf16[3072,128]{1,0:T(8,128)(2,1)S(1)} %bitcast.55, f32[48,128]{1,0:T(8,128)S(1)} %copy-done.1, f32[48,128]{1,0:T(8,128)S(1)} %copy-done.2, f32[48,128]{1,0:T(8,128)S(1)} %copy-done.3, f32[48,128]{1,0:T(8,128)S(1)} %copy-done.4, f32[32,128]{1,0:T(8,128)S(1)} %copy-done.5, f32[32,128]{1,0:T(8,128)S(1)} %copy-done.6), custom_call_target="tpu_custom_call" | custom-call | tf_op jit(solution)/shard_map/hartley/pallas_call | solution.py:168
  80.2 24.1 %all_to_all.29 = bf16[24,64,128]{2,1,0:T(8,128)(2,1)S(1)} all-to-all(bf16[24,64,128]{2,1,0:T(8,128)(2,1)S(1)} %bitcast.57), channel_id=1, replica_groups=mesh['lat'=32,'lon'=24] {'lon'}, dimensions={0} | all-to-all | bytes 786432 | tf_op jit(solution)/shard_map/all_to_all | solution.py:193
  104.3 1.0 copy.33
  105.3 10.2 %all-to-all-start.2 = ((bf16[24,64,128]{2,0,1:T(8,128)(2,1)}), bf16[24,64,128]{2,0,1:T(8,128)(2,1)S(1)}, u32[]{:S(2)}, u32[]{:S(2)}) async-start(bf16[24,64,128]{2,0,1:T(8,128)(2,1)} %copy.33), calls=%async_computation.2 | async-start | bytes 786432 | tf_op jit(solution)/shard_map/all_to_all | solution.py:196
  115.5 12.8 %all-to-all-done.2 = bf16[24,64,128]{2,0,1:T(8,128)(2,1)S(1)} async-done(((bf16[24,64,128]{2,0,1:T(8,128)(2,1)}), bf16[24,64,128]{2,0,1:T(8,128)(2,1)S(1)}, u32[]{:S(2)}, u32[]{:S(2)}) %all-to-all-start.2) | async-done | bytes 393248 | tf_op jit(solution)/shard_map/all_to_all | solution.py:196
  128.3 0.0 copy-done
  128.3 0.5 fusion
  128.8 1.1 copy.36
  (5 shorter events, 0.1 us)
Async XLA Ops:
  0.0 128.3 %copy-start = (bf16[2,768,768]{2,1,0:T(8,128)(2,1)S(1)}, bf16[2,768,768]{2,1,0:T(8,128)(2,1)}, u32[]{:S(2)}) copy-start(bf16[2,768,768]{2,1,0:T(8,128)(2,1)} %param.17) | copy-start | bytes 7077892
  1.6 21.9 %collective-permute-start = (bf16[192,2048]{1,0:T(8,128)(2,1)S(1)}, bf16[192,2048]{1,0:T(8,128)(2,1)}, u32[]{:S(2)}, u32[]{:S(2)}) collective-permute-start(bf16[192,2048]{1,0:T(8,128)(2,1)S(1)} %reshape.47.own_ref), channel_id=1, source_target_pairs={{0,1},{1,2},{2,3},{3,4},{4,5},{5,6},{6,7},{7,8},{8,9},{9,10},{10,1... | collective-permute-start | bytes 2359304 | tf_op jit(solution)/shard_map/ppermute | solution.py:187
  1.6 21.9 %collective-permute-start.1 = (bf16[192,2048]{1,0:T(8,128)(2,1)S(1)}, bf16[192,2048]{1,0:T(8,128)(2,1)}, u32[]{:S(2)}, u32[]{:S(2)}) collective-permute-start(bf16[192,2048]{1,0:T(8,128)(2,1)S(1)} %reshape.47.own_ref), channel_id=1, source_target_pairs={{1,0},{2,1},{3,2},{4,3},{5,4},{6,5},{7,6},{8,7},{9,8},{10,9},{11,1... | collective-permute-start | bytes 2359304 | tf_op jit(solution)/shard_map/ppermute | solution.py:188
  22.1 52.4 %copy-start.1 = (f32[48,128]{1,0:T(8,128)S(1)}, f32[48,128]{1,0:T(8,128)}, u32[]{:S(2)}) copy-start(f32[48,128]{1,0:T(8,128)} %constant.36.clone.refs_0_) | copy-start | bytes 73732
  22.1 52.4 %copy-start.2 = (f32[48,128]{1,0:T(8,128)S(1)}, f32[48,128]{1,0:T(8,128)}, u32[]{:S(2)}) copy-start(f32[48,128]{1,0:T(8,128)} %constant.37.clone.refs_1_) | copy-start | bytes 73732
  22.1 52.4 %copy-start.3 = (f32[48,128]{1,0:T(8,128)S(1)}, f32[48,128]{1,0:T(8,128)}, u32[]{:S(2)}) copy-start(f32[48,128]{1,0:T(8,128)} %constant.38.clone.refs_2_) | copy-start | bytes 73732
  22.1 52.4 %copy-start.4 = (f32[48,128]{1,0:T(8,128)S(1)}, f32[48,128]{1,0:T(8,128)}, u32[]{:S(2)}) copy-start(f32[48,128]{1,0:T(8,128)} %constant.39.clone.refs_3_) | copy-start | bytes 73732
  22.1 52.4 %copy-start.5 = (f32[32,128]{1,0:T(8,128)S(1)}, f32[32,128]{1,0:T(8,128)}, u32[]{:S(2)}) copy-start(f32[32,128]{1,0:T(8,128)} %constant.40.clone.refs_4_) | copy-start | bytes 49156
  22.1 52.4 %copy-start.6 = (f32[32,128]{1,0:T(8,128)S(1)}, f32[32,128]{1,0:T(8,128)}, u32[]{:S(2)}) copy-start(f32[32,128]{1,0:T(8,128)} %constant.41.clone.refs_5_) | copy-start | bytes 49156
  105.3 22.9 %all-to-all-start.2 = ((bf16[24,64,128]{2,0,1:T(8,128)(2,1)}), bf16[24,64,128]{2,0,1:T(8,128)(2,1)S(1)}, u32[]{:S(2)}, u32[]{:S(2)}) async-start(bf16[24,64,128]{2,0,1:T(8,128)(2,1)} %copy.33), calls=%async_computation.2 | async-start | bytes 786432 | tf_op jit(solution)/shard_map/all_to_all | solution.py:196

commit v2 on v1

--- a/solution.py
+++ b/solution.py
@@ -18,6 +18,8 @@
 NLON = 3072
 BLOCKS = COLS // BLK
 FINE = 48
+CHUNK = 4
+MESH = pl.DeviceIdType.MESH
 
 
 def small_tables():
@@ -85,46 +87,6 @@
         weight_ref[here, :] = weight
 
 
-def interpolate_kernel(ends_ref, cells_ref, left_ref, own_ref, right_ref, out_ref, tiles, onehot, weight):
-    tiles[:BLOCKS, :] = left_ref[...]
-    tiles[BLOCKS : 2 * BLOCKS, :] = own_ref[...]
-    tiles[2 * BLOCKS :, :] = right_ref[...]
-    decode(ends_ref, cells_ref, onehot, weight)
-    step = 512
-    for half in range(2):
-        low = half * BLOCKS
-        for part in range(COLS // 2 // step):
-            here = pl.ds(half * (COLS // 2) + part * step, step)
-            total = jnp.zeros((step, 128), jnp.float32)
-            for pair in range(BLK // 2):
-                got = jnp.dot(
-                    onehot[here, :],
-                    tiles[low : low + 2 * BLOCKS, pair * 256 : (pair + 1) * 256],
-                    preferred_element_type=jnp.float32,
-                )
-                scale = weight[here, :]
-                total = total + scale[:, 2 * pair : 2 * pair + 1] * got[:, :128]
-                total = total + scale[:, 2 * pair + 1 : 2 * pair + 2] * got[:, 128:]
-            out_ref[here, :] = total.astype(jnp.bfloat16)
-
-
-def interpolate(ends, cells, left, own, right):
-    vmem = pl.BlockSpec(memory_space=pltpu.VMEM)
-    return pl.pallas_call(
-        interpolate_kernel,
-        out_shape=jax.ShapeDtypeStruct((COLS, 128), jnp.bfloat16),
-        in_specs=[pl.BlockSpec(memory_space=pltpu.SMEM), vmem, vmem, vmem, vmem],
-        out_specs=vmem,
-        scratch_shapes=[
-            pltpu.VMEM((3 * BLOCKS, BLK * 128), jnp.bfloat16),
-            pltpu.VMEM((COLS, 2 * BLOCKS), jnp.bfloat16),
-            pltpu.VMEM((COLS, 128), jnp.float32),
-        ],
-        compiler_params=pltpu.CompilerParams(vmem_limit_bytes=40 << 20),
-        name="interpolate",
-    )(ends, cells, left, own, right)
-
-
 def fill_table(small, plus, minus, table):
     near_plus, near_minus, far_cos, far_sin, coarse_cos, coarse_sin = small
     for sector in range(NLON // 128):
@@ -148,53 +110,237 @@
     lax.fori_loop(0, KF // FINE, body, 0)
 
 
-def hartley_kernel(rows_ref, *refs):
-    small, out_ref, plus, minus, table = refs[:6], refs[6], refs[7], refs[8], refs[9]
-    fill_table(small, plus, minus, table)
-    step = 512
-    for part in range(KF // step):
-        total = jnp.zeros((step, 128), jnp.float32)
-        for pair in range(NLON // 256):
-            total = total + jnp.dot(
-                table[pair, part * step : (part + 1) * step, :],
-                rows_ref[pair * 256 : (pair + 1) * 256, :],
+def ring_offset(step, count):
+    return jnp.where(step % 2 == 1, (step + 1) // 2, count - step // 2)
+
+
+def transform_kernel(
+    lon,
+    lat,
+    ends_ref,
+    cells_ref,
+    left_ref,
+    own_ref,
+    right_ref,
+    *refs,
+):
+    small, out_ref = refs[:6], refs[6]
+    (tiles, onehot, weight, departed, sectors, plus, minus, table, total, blocks, landed, wide, packs, bands) = refs[7:21]
+    send_row, recv_row, send_block, recv_block, send_band, recv_band = refs[21:]
+    me_lon, me_lat = lax.axis_index("lon"), lax.axis_index("lat")
+    rows = departed.shape[0]
+    depth = blocks.shape[1]
+    each = depth // lat
+    chips = lon // 2
+
+    barrier = pltpu.get_barrier_semaphore()
+
+    def greet_lon(step, carry):
+        peer = lax.rem(me_lon + step, lon)
+        pl.semaphore_signal(barrier, inc=1, device_id={"lon": peer}, device_id_type=MESH)
+        return carry
+
+    def greet_lat(step, carry):
+        peer = lax.rem(me_lat + step, lat)
+        pl.semaphore_signal(barrier, inc=1, device_id={"lat": peer}, device_id_type=MESH)
+        return carry
+
+    lax.fori_loop(1, lon, greet_lon, 0)
+    lax.fori_loop(1, lat, greet_lat, 0)
+
+    tiles[:BLOCKS, :] = left_ref[...]
+    tiles[BLOCKS : 2 * BLOCKS, :] = own_ref[...]
+    tiles[2 * BLOCKS :, :] = right_ref[...]
+    decode(ends_ref, cells_ref, onehot, weight)
+    pl.semaphore_wait(barrier, lon + lat - 2)
+
+    def row_copy(source, row, slot_send, slot_recv):
+        return pltpu.make_async_remote_copy(
+            src_ref=departed.at[row],
+            dst_ref=sectors.at[source // 2, pl.ds(pl.multiple_of((source % 2) * 128, 128), 128), :],
+            send_sem=send_row.at[slot_send],
+            recv_sem=recv_row.at[slot_recv],
+            device_id={"lon": row},
+            device_id_type=MESH,
+        )
+
+    step = CHUNK * 128
+    for part in range(rows // CHUNK):
+        low = 0 if part * CHUNK < rows // 2 else BLOCKS
+        here = pl.ds(part * step, step)
+        values = jnp.zeros((step, 128), jnp.float32)
+        for pair in range(BLK // 2):
+            got = jnp.dot(
+                onehot[here, :],
+                tiles[low : low + 2 * BLOCKS, pair * 256 : (pair + 1) * 256],
                 preferred_element_type=jnp.float32,
             )
-        out_ref[part * step : (part + 1) * step, :] = total.astype(jnp.bfloat16)
-
-
-def hartley(rows):
+            scale = weight[here, :]
+            values = values + scale[:, 2 * pair : 2 * pair + 1] * got[:, :128]
+            values = values + scale[:, 2 * pair + 1 : 2 * pair + 2] * got[:, 128:]
+        departed[part * CHUNK : (part + 1) * CHUNK] = values.astype(jnp.bfloat16).reshape(CHUNK, 128, 128)
+
+        def send_rows(row, carry):
+            @pl.when(row != me_lon)
+            def _():
+                row_copy(me_lon, row, row, me_lon).start()
+
+            return carry
+
+        lax.fori_loop(part * CHUNK, (part + 1) * CHUNK, send_rows, 0)
+
+    sectors[me_lon // 2, pl.ds(pl.multiple_of((me_lon % 2) * 128, 128), 128), :] = departed[me_lon]
+    fill_table(small, plus, minus, table)
+    total[...] = jnp.zeros_like(total)
+
+    def gather_chip(chip):
+        for core in range(2):
+            source = chip * 2 + core
+
+            @pl.when(source != me_lon)
+            def _():
+                row_copy(source, 0, source, source).wait_recv()
+
+    def accumulate(step, carry):
+        chip = lax.rem(me_lon // 2 + ring_offset(step, chips), chips)
+        gather_chip(chip)
+        for part in range(3):
+            here = slice(part * (KF // 3), (part + 1) * (KF // 3))
+            total[here, :] += jnp.dot(table[chip, here, :], sectors[chip], preferred_element_type=jnp.float32)
+        return carry
+
+    lax.fori_loop(0, chips, accumulate, 0)
+
+    def block_copy(source, block, slot_send, slot_recv):
+        return pltpu.make_async_remote_copy(
+            src_ref=blocks.at[block],
+            dst_ref=landed.at[source],
+            send_sem=send_block.at[slot_send],
+            recv_sem=recv_block.at[slot_recv],
+            device_id={"lon": block},
+            device_id_type=MESH,
+        )
+
+    blocks[...] = total[...].astype(jnp.bfloat16).reshape(blocks.shape)
+
+    def send_blocks(step, carry):
+        block = lax.rem(me_lon + step, lon)
+        block_copy(me_lon, block, block, me_lon).start()
+        return carry
+
+    lax.fori_loop(1, lon, send_blocks, 0)
+    wide[pl.ds(pl.multiple_of(me_lon * depth, depth), depth), :] = blocks[me_lon].astype(jnp.float32)
+
+    def widen(step, carry):
+        chip = lax.rem(me_lon // 2 + ring_offset(step, chips), chips)
+        for core in range(2):
+            source = chip * 2 + core
+
+            @pl.when(source != me_lon)
+            def _():
+                block_copy(source, 0, source, source).wait_recv()
+                wide[pl.ds(pl.multiple_of(source * depth, depth), depth), :] = landed[source].astype(jnp.float32)
+
+        return carry
+
+    lax.fori_loop(0, chips, widen, 0)
+
+    def band_copy(source, target, slot_send, slot_recv):
+        return pltpu.make_async_remote_copy(
+            src_ref=packs.at[target],
+            dst_ref=bands.at[source],
+            send_sem=send_band.at[slot_send],
+            recv_sem=recv_band.at[slot_recv],
+            device_id={"lat": target},
+            device_id_type=MESH,
+        )
+
+    def send_bands(step, carry):
+        target = lax.rem(me_lat + step, lat)
+        picked = [wide[pl.ds(target * each + k, lon, stride=depth), :] for k in range(each)]
+        packs[target] = jnp.concatenate(picked, axis=0).astype(jnp.bfloat16)
+
+        @pl.when(target != me_lat)
+        def _():
+            band_copy(me_lat, target, target, me_lat).start()
+
+        return carry
+
+    lax.fori_loop(1, lat + 1, send_bands, 0)
+    bands[me_lat] = packs[me_lat]
+
+    def finish_rows(step, carry):
+        peer = lax.rem(me_lon + step, lon)
+        row_copy(me_lon, peer, peer, me_lon).wait_send()
+        block_copy(me_lon, peer, peer, me_lon).wait_send()
+        return carry
+
+    lax.fori_loop(1, lon, finish_rows, 0)
+
+    def finish_bands(step, carry):
+        peer = lax.rem(me_lat + step, lat)
+        band_copy(peer, 0, peer, peer).wait_recv()
+        band_copy(me_lat, peer, peer, me_lat).wait_send()
+        return carry
+
+    lax.fori_loop(1, lat, finish_bands, 0)
+    out_ref[...] = bands[...]
+
+
+def transform(lon, lat, ends, cells, left, own, right):
     vmem = pl.BlockSpec(memory_space=pltpu.VMEM)
+    depth = KF // lon
+    band = (lat, depth // lat * lon, 128)
     return pl.pallas_call(
-        hartley_kernel,
-        out_shape=jax.ShapeDtypeStruct((KF, 128), jnp.bfloat16),
-        in_specs=[vmem] * 7,
+        functools.partial(transform_kernel, lon, lat),
+        out_shape=jax.ShapeDtypeStruct(band, jnp.bfloat16),
+        in_specs=[pl.BlockSpec(memory_space=pltpu.SMEM)] + [vmem] * 10,
         out_specs=vmem,
         scratch_shapes=[
+            pltpu.VMEM((3 * BLOCKS, BLK * 128), jnp.bfloat16),
+            pltpu.VMEM((COLS, 2 * BLOCKS), jnp.bfloat16),
+            pltpu.VMEM((COLS, 128), jnp.float32),
+            pltpu.VMEM((COLS // 128, 128, 128), jnp.bfloat16),
+            pltpu.VMEM((lon // 2, 256, 128), jnp.bfloat16),
             pltpu.VMEM((FINE, NLON), jnp.float32),
             pltpu.VMEM((FINE, NLON), jnp.float32),
             pltpu.VMEM((NLON // 256, KF, 256), jnp.bfloat16),
+            pltpu.VMEM((KF, 128), jnp.float32),
+            pltpu.VMEM((lon, depth, 128), jnp.bfloat16),
+            pltpu.VMEM((lon, depth, 128), jnp.bfloat16),
+            pltpu.VMEM((lon * depth, 128), jnp.float32),
+            pltpu.VMEM(band, jnp.bfloat16),
+            pltpu.VMEM(band, jnp.bfloat16),
+            pltpu.SemaphoreType.DMA((lon,)),
+            pltpu.SemaphoreType.DMA((lon,)),
+            pltpu.SemaphoreType.DMA((lon,)),
+            pltpu.SemaphoreType.DMA((lon,)),
+            pltpu.SemaphoreType.DMA((lat,)),
+            pltpu.SemaphoreType.DMA((lat,)),
         ],
-        compiler_params=pltpu.CompilerParams(vmem_limit_bytes=40 << 20),
-        name="hartley",
-    )(rows, *small_tables())
-
-
-def local(fields, req_block, req_stencil, req_frac, req_count, legendre):
+        compiler_params=pltpu.CompilerParams(
+            vmem_limit_bytes=48 << 20, collective_id=0, has_side_effects=True
+        ),
+        name="transform",
+    )(ends, cells, left, own, right, *small_tables())
+
+
+def gathered_bands(fields, req_block, req_stencil, req_frac, req_count):
     lon = lax.axis_size("lon")
     lat = lax.axis_size("lat")
     tile = fields.reshape(BLOCKS, BLK * 128)
     left = lax.ppermute(tile, "lon", [(i, (i + 1) % lon) for i in range(lon)])
     right = lax.ppermute(tile, "lon", [((i + 1) % lon, i) for i in range(lon)])
     cells, ends = cell_requests(req_block[0, 0], req_stencil[0, 0], req_frac[0, 0], req_count[0, 0])
-    departed = interpolate(ends, cells, left, tile, right)
-    rows = lax.all_to_all(departed.reshape(24, 128, 128), "lon", split_axis=0, concat_axis=0, tiled=True)
-    spectra = hartley(rows.reshape(NLON, 128))
-    fourier = lax.all_to_all(
-        spectra.reshape(lon, KF // lon, 128), "lon", split_axis=0, concat_axis=0, tiled=True
-    )
-    gathered = lax.all_to_all(fourier, "lat", split_axis=1, concat_axis=0, tiled=True)
-    projected = jnp.einsum("kyn,ykc->knc", legendre, gathered, preferred_element_type=jnp.float32)
+    bands = transform(lon, lat, ends, cells, left, tile, right)
+    own = KF // lon // lat
+    bands = bands.reshape(lat, own, lon, 128).transpose(1, 0, 2, 3)
+    return bands.reshape(own, lat * lon, 128)
+
+
+def local(fields, req_block, req_stencil, req_frac, req_count, legendre):
+    gathered = gathered_bands(fields, req_block, req_stencil, req_frac, req_count)
+    projected = jnp.einsum("kyn,kyc->knc", legendre, gathered, preferred_element_type=jnp.float32)
     degree = jnp.arange(NN, dtype=jnp.float32)
     factor = 1.0 / (1.0 + 4.0 * degree * (degree + 1.0) / (NN * (NN + 1)))
     return projected * factor[None, :, None]

time: 130 us -> 111 us (0.85)
  the two profiles are of different devices: /device:TPU:8 before, /device:TPU:1 now
where the time goes in v2:
time: 111 us
  Pallas kernels  84.4 us (76%)
  local copies, waits for them, and re-layouts  10.8 us (10%)
  starting transfers between devices  10.5 us (9%)
  between operations  2.94 us (3%)
  other arithmetic  1.38 us (1%)
    pallas_call x1, Pallas kernels, transform(): pl.pallas_call(functools.partial(transform_kernel, lon, lat), out_shape=j...  84.4 us
    ppermute x1, starting transfers between devices, gathered_bands(): right = lax.ppermute(tile, 'lon', [((i + 1) % lon, i) for i in range(lon)])  7.04 us
    unnamed x15, local copies, waits for them, and re-layouts  5.23 us
    ppermute x1, starting transfers between devices, gathered_bands(): left = lax.ppermute(tile, 'lon', [(i, (i + 1) % lon) for i in range(lon)])  3.49 us
  transfers between devices with their start and end apart: 2, of which 0 were waited for; matrix products, arithmetic and copies ran while one was open for 5% of the time, Pallas kernels for 0%

profile of v2, /device:TPU:1, one launch (start us, length us, event | category | flops | bytes accessed | tf_op | source)
XLA Modules:
  0.0 110.6 jit_solution(13432089115095049938)
XLA Ops:
  0.0 0.0 copy-start
  0.0 1.6 %reshape.44.own_ref = bf16[192,2048]{1,0:T(8,128)(2,1)S(1)} reshape(bf16[24,128,128]{2,1,0:T(8,128)(2,1)} %param.12) | data formatting | bytes 1572864 | tf_op jit(solution)/shard_map/reshape | solution.py:331
  1.6 3.5 %collective-permute-start = (bf16[192,2048]{1,0:T(8,128)(2,1)S(1)}, bf16[192,2048]{1,0:T(8,128)(2,1)}, u32[]{:S(2)}, u32[]{:S(2)}) collective-permute-start(bf16[192,2048]{1,0:T(8,128)(2,1)S(1)} %reshape.44.own_ref), channel_id=1, source_target_pairs={{0,1},{1,2},{2,3},{3,4},{4,5},{5,6},{6,7},{7,8},{8,9},{9,10},{10,1... | collective-permute-start | bytes 2359304 | tf_op jit(solution)/shard_map/ppermute | solution.py:332
  5.1 7.0 %collective-permute-start.1 = (bf16[192,2048]{1,0:T(8,128)(2,1)S(1)}, bf16[192,2048]{1,0:T(8,128)(2,1)}, u32[]{:S(2)}, u32[]{:S(2)}) collective-permute-start(bf16[192,2048]{1,0:T(8,128)(2,1)S(1)} %reshape.44.own_ref), channel_id=1, source_target_pairs={{1,0},{2,1},{3,2},{4,3},{5,4},{6,5},{7,6},{8,7},{9,8},{10,9},{11,1... | collective-permute-start | bytes 2359304 | tf_op jit(solution)/shard_map/ppermute | solution.py:333
  12.1 0.9 fusion.16
  13.0 0.9 copy.37
  13.8 0.7 fusion.4
  14.6 1.3 %fusion.17 = (s32[1,1,1]{2,1,0:T(1,128)}, s32[1,1,1]{2,1,0:T(1,128)}) fusion(s32[1,1,3]{2,1,0:T(1,128)} %param.16), kind=kLoop, calls=%fused_computation.32 | loop fusion | bytes 16 | tf_op jit(solution)/shard_map/slice | solution.py:50
  18.8 0.3 dynamic_update_slice.10
  19.1 0.3 dynamic_update_slice.11
  19.4 0.6 pad_add_fusion.ends_ref
  20.1 0.0 collective-permute-done.left_ref
  20.1 0.0 collective-permute-done.1.right_ref
  20.1 0.0 copy-start.1
  20.1 0.7 copy-done.1
  20.8 0.0 copy-start.2
  20.8 0.7 copy-done.2
  21.6 0.0 copy-start.3
  21.6 0.7 copy-done.3
  22.3 0.0 copy-start.4
  22.3 0.7 copy-done.4
  23.0 0.0 copy-start.5
  23.0 0.7 copy-done.5
  23.7 0.0 copy-start.6
  23.7 0.7 copy-done.6
  24.5 84.4 %transform.1 = bf16[32,48,128]{2,1,0:T(8,128)(2,1)S(1)} custom-call(s32[2]{0:T(128)S(1)} %pad_add_fusion.ends_ref, s32[24,128]{1,0:T(8,128)S(1)} %slice_bitcast_fusion.cells_ref, bf16[192,2048]{1,0:T(8,128)(2,1)} %collective-permute-done.left_ref, bf16[192,2048]{1,0:T(8,128)(2,1)S(1)} %reshape.44.own_ref, ...), custom_call_target="tpu_custom_call" | custom-call | tf_op jit(solution)/shard_map/transform/pallas_call | solution.py:294
  108.9 0.0 copy-done
  108.9 0.5 fusion
  109.4 1.1 %copy.23 = f32[2,768,128]{2,1,0:T(8,128)} copy(f32[2,768,128]{1,2,0:T(8,128)S(1)} %fusion) | data formatting | bytes 1572864 | tf_op jit(solution)/shard_map/mul | solution.py:346
  (5 shorter events, 0.1 us)
Async XLA Ops:
  0.0 108.9 %copy-start = (bf16[2,768,768]{2,1,0:T(8,128)(2,1)S(1)}, bf16[2,768,768]{2,1,0:T(8,128)(2,1)}, u32[]{:S(2)}) copy-start(bf16[2,768,768]{2,1,0:T(8,128)(2,1)} %param.17) | copy-start | bytes 7077892
  1.6 18.5 %collective-permute-start = (bf16[192,2048]{1,0:T(8,128)(2,1)S(1)}, bf16[192,2048]{1,0:T(8,128)(2,1)}, u32[]{:S(2)}, u32[]{:S(2)}) collective-permute-start(bf16[192,2048]{1,0:T(8,128)(2,1)S(1)} %reshape.44.own_ref), channel_id=1, source_target_pairs={{0,1},{1,2},{2,3},{3,4},{4,5},{5,6},{6,7},{7,8},{8,9},{9,10},{10,1... | collective-permute-start | bytes 2359304 | tf_op jit(solution)/shard_map/ppermute | solution.py:332
  5.1 15.0 %collective-permute-start.1 = (bf16[192,2048]{1,0:T(8,128)(2,1)S(1)}, bf16[192,2048]{1,0:T(8,128)(2,1)}, u32[]{:S(2)}, u32[]{:S(2)}) collective-permute-start(bf16[192,2048]{1,0:T(8,128)(2,1)S(1)} %reshape.44.own_ref), channel_id=1, source_target_pairs={{1,0},{2,1},{3,2},{4,3},{5,4},{6,5},{7,6},{8,7},{9,8},{10,9},{11,1... | collective-permute-start | bytes 2359304 | tf_op jit(solution)/shard_map/ppermute | solution.py:333
  20.1 0.7 copy-start.1
  20.8 0.7 copy-start.2
  21.6 0.7 copy-start.3
  22.3 0.7 copy-start.4
  23.0 0.7 copy-start.5
  23.7 0.7 copy-start.6

commit v3 on v2

--- a/solution.py
+++ b/solution.py
@@ -33,29 +33,48 @@
     far = unit * (fine * lane * 128 % NLON)
     coarse = unit * (np.arange(KF // FINE, dtype=np.int64)[:, None] * FINE * lane % NLON)
     tables = [plus, minus, np.cos(far), np.sin(far), np.cos(coarse), np.sin(coarse)]
-    return [np.asarray(t, dtype=np.float32) for t in tables]
-
-
-def cell_requests(req_block, req_stencil, req_frac, counts):
-    packed = (
-        (req_block << 24)
-        | (req_stencil[:, 0] << 20)
-        | (req_stencil[:, 1] << 16)
-        | (req_stencil[:, 2] << 12)
-        | (req_stencil[:, 3] << 8)
-        | (req_frac[:, 0] << 4)
-        | req_frac[:, 1]
-    )
-    first = counts[0]
-    second = first + counts[1]
-    cells = jnp.zeros((COLS + CAP,), jnp.int32)
-    cells = lax.dynamic_update_slice(cells, packed[0], (0,))
-    cells = lax.dynamic_update_slice(cells, packed[1], (first,))
-    cells = lax.dynamic_update_slice(cells, packed[2], (second,))
-    return cells[:COLS].reshape(COLS // 128, 128), jnp.stack([first, second])
-
-
-def decode(ends_ref, cells_ref, onehot_ref, weight_ref):
+    return np.concatenate(tables, axis=0).astype(np.float32)
+
+
+def order_kernel(count_ref, block_ref, stencil_ref, frac_ref, cells_ref):
+    first = count_ref[0]
+    second = first + count_ref[1]
+    lane = lax.broadcasted_iota(jnp.int32, (32, 128), 1)
+    cell = lax.broadcasted_iota(jnp.int32, (32, 128), 0) * 128 + lane
+    result = None
+    for slot, start in ((0, None), (1, first), (2, second)):
+        shift4 = 20 - 4 * lax.broadcasted_iota(jnp.int32, (4, CAP), 0)
+        shift2 = 4 - 4 * lax.broadcasted_iota(jnp.int32, (2, CAP), 0)
+        word = (
+            lax.shift_left(block_ref[slot : slot + 1, :], jnp.full((1, CAP), 24, jnp.int32))
+            + jnp.sum(lax.shift_left(stencil_ref[slot], shift4), axis=0, keepdims=True)
+            + jnp.sum(lax.shift_left(frac_ref[slot], shift2), axis=0, keepdims=True)
+        )
+        pieces = [word[:, k * 128 : (k + 1) * 128] for k in range(CAP // 128)]
+        pieces.append(jnp.zeros((32 - CAP // 128, 128), jnp.int32))
+        placed = jnp.concatenate(pieces, axis=0)
+        if start is None:
+            result = placed
+            continue
+        turn = start % 128
+        turned = pltpu.roll(placed, turn, 1)
+        turned = jnp.where(lane < turn, pltpu.roll(turned, 1, 0), turned)
+        result = jnp.where(cell < start, result, pltpu.roll(turned, start // 128, 0))
+    cells_ref[...] = result[: cells_ref.shape[0], :]
+
+
+def order_requests(count, block, stencil, frac):
+    vmem = pl.BlockSpec(memory_space=pltpu.VMEM)
+    return pl.pallas_call(
+        order_kernel,
+        out_shape=jax.ShapeDtypeStruct((COLS // 128, 128), jnp.int32),
+        in_specs=[pl.BlockSpec(memory_space=pltpu.SMEM), vmem, vmem, vmem],
+        out_specs=vmem,
+        name="order_requests",
+    )(count, block, stencil, frac)
+
+
+def decode(first, second, cells_ref, onehot_ref, weight_ref):
     rows = cells_ref.shape[0]
     columns = jnp.concatenate(
         [cells_ref[...], jnp.zeros((128 - rows, 128), jnp.int32)], axis=0
@@ -65,7 +84,7 @@
     for row in range(rows):
         word = jnp.broadcast_to(columns[:, row : row + 1], (128, 128))
         block = lax.shift_right_logical(word, 24)
-        edge = ends_ref[0] if row < rows // 2 else ends_ref[1]
+        edge = first if row < rows // 2 else second
         block = block + jnp.where(sub + row * 128 >= edge, BLOCKS, 0)
         here = pl.ds(row * 128, 128)
         for part in range(3):
@@ -88,7 +107,8 @@
 
 
 def fill_table(small, plus, minus, table):
-    near_plus, near_minus, far_cos, far_sin, coarse_cos, coarse_sin = small
+    near_plus, near_minus, far_cos, far_sin = [small.at[pl.ds(k * FINE, FINE)] for k in range(4)]
+    coarse_cos, coarse_sin = [small.at[pl.ds(4 * FINE + k * (KF // FINE), KF // FINE)] for k in range(2)]
     for sector in range(NLON // 128):
         here = pl.ds(sector * 128, 128)
         turn_cos = far_cos[:, sector : sector + 1]
@@ -110,28 +130,26 @@
     lax.fori_loop(0, KF // FINE, body, 0)
 
 
-def ring_offset(step, count):
+def near_first(step, count):
     return jnp.where(step % 2 == 1, (step + 1) // 2, count - step // 2)
 
 
-def transform_kernel(
-    lon,
-    lat,
-    ends_ref,
-    cells_ref,
-    left_ref,
-    own_ref,
-    right_ref,
-    *refs,
-):
-    small, out_ref = refs[:6], refs[6]
-    (tiles, onehot, weight, departed, sectors, plus, minus, table, total, blocks, landed, wide, packs, bands) = refs[7:21]
-    send_row, recv_row, send_block, recv_block, send_band, recv_band = refs[21:]
+def far_first(step, count):
+    away = count // 2 - (step + 1) // 2
+    return jnp.where(step % 2 == 1, away, count - away)
+
+
+def transform_kernel(lon, lat, count_hbm, cells_hbm, own_hbm, table_ref, out_ref, *refs):
+    (count_ref, cells_ref, own_ref, small, tiles, onehot, weight, departed, sectors, plus, minus, table, total, blocks, landed, wide, packs, bands) = refs[:18]
+    fetch_sem, send_tile, recv_tile, send_row, recv_row, send_block, recv_block, send_band, recv_band = refs[18:]
     me_lon, me_lat = lax.axis_index("lon"), lax.axis_index("lat")
     rows = departed.shape[0]
     depth = blocks.shape[1]
     each = depth // lat
     chips = lon // 2
+    me_chip = me_lon // 2
+    tall = 8 if lat == 32 else lat
+    flat = lat // tall
 
     barrier = pltpu.get_barrier_semaphore()
 
@@ -147,12 +165,39 @@
 
     lax.fori_loop(1, lon, greet_lon, 0)
     lax.fori_loop(1, lat, greet_lat, 0)
-
-    tiles[:BLOCKS, :] = left_ref[...]
-    tiles[BLOCKS : 2 * BLOCKS, :] = own_ref[...]
-    tiles[2 * BLOCKS :, :] = right_ref[...]
-    decode(ends_ref, cells_ref, onehot, weight)
+    pairs = ((own_hbm, own_ref), (count_hbm, count_ref), (cells_hbm, cells_ref), (table_ref, small))
+    fetches = [pltpu.make_async_copy(src, dst, fetch_sem.at[k]) for k, (src, dst) in enumerate(pairs)]
+    for fetch in fetches:
+        fetch.start()
+    fetches[0].wait()
+
+    weight[...] = own_ref[...].astype(jnp.float32)
+    for cell in range(BLK):
+        tiles[BLOCKS : 2 * BLOCKS, cell * 128 : (cell + 1) * 128] = weight[
+            pl.ds(cell, BLOCKS, stride=BLK), :
+        ].astype(jnp.bfloat16)
     pl.semaphore_wait(barrier, lon + lat - 2)
+
+    def tile_copy(side):
+        return pltpu.make_async_remote_copy(
+            src_ref=tiles.at[pl.ds(BLOCKS, BLOCKS)],
+            dst_ref=tiles.at[pl.ds(2 * BLOCKS * side, BLOCKS)],
+            send_sem=send_tile.at[side],
+            recv_sem=recv_tile.at[side],
+            device_id={"lon": lax.rem(me_lon + (1 if side == 0 else lon - 1), lon)},
+            device_id_type=MESH,
+        )
+
+    for side in range(2):
+        tile_copy(side).start()
+    fetches[1].wait()
+    fetches[2].wait()
+    decode(count_ref[0], count_ref[0] + count_ref[1], cells_ref, onehot, weight)
+    fetches[3].wait()
+    fill_table(small, plus, minus, table)
+    total[...] = jnp.zeros_like(total)
+    for side in range(2):
+        tile_copy(side).wait_recv()
 
     def row_copy(source, row, slot_send, slot_recv):
         return pltpu.make_async_remote_copy(
@@ -164,36 +209,39 @@
             device_id_type=MESH,
         )
 
-    step = CHUNK * 128
-    for part in range(rows // CHUNK):
-        low = 0 if part * CHUNK < rows // 2 else BLOCKS
-        here = pl.ds(part * step, step)
-        values = jnp.zeros((step, 128), jnp.float32)
+    parts = rows // CHUNK
+
+    def interpolate(turn, carry):
+        part = lax.rem(me_lon // CHUNK + far_first(turn, parts), parts)
+        low = pl.multiple_of(jnp.where(part < parts // 2, 0, BLOCKS), BLOCKS)
+        here = pl.ds(pl.multiple_of(part * CHUNK * 128, CHUNK * 128), CHUNK * 128)
+        values = jnp.zeros((CHUNK * 128, 128), jnp.float32)
         for pair in range(BLK // 2):
             got = jnp.dot(
                 onehot[here, :],
-                tiles[low : low + 2 * BLOCKS, pair * 256 : (pair + 1) * 256],
+                tiles[pl.ds(low, 2 * BLOCKS), pair * 256 : (pair + 1) * 256],
                 preferred_element_type=jnp.float32,
             )
             scale = weight[here, :]
             values = values + scale[:, 2 * pair : 2 * pair + 1] * got[:, :128]
             values = values + scale[:, 2 * pair + 1 : 2 * pair + 2] * got[:, 128:]
-        departed[part * CHUNK : (part + 1) * CHUNK] = values.astype(jnp.bfloat16).reshape(CHUNK, 128, 128)
-
-        def send_rows(row, carry):
+        departed[pl.ds(part * CHUNK, CHUNK)] = values.astype(jnp.bfloat16).reshape(CHUNK, 128, 128)
+
+        def send_rows(row, inner):
             @pl.when(row != me_lon)
             def _():
                 row_copy(me_lon, row, row, me_lon).start()
 
-            return carry
-
-        lax.fori_loop(part * CHUNK, (part + 1) * CHUNK, send_rows, 0)
-
-    sectors[me_lon // 2, pl.ds(pl.multiple_of((me_lon % 2) * 128, 128), 128), :] = departed[me_lon]
-    fill_table(small, plus, minus, table)
-    total[...] = jnp.zeros_like(total)
-
-    def gather_chip(chip):
+            return inner
+
+        lax.fori_loop(part * CHUNK, part * CHUNK + CHUNK, send_rows, 0)
+        return carry
+
+    lax.fori_loop(0, parts, interpolate, 0)
+    sectors[me_chip, pl.ds(pl.multiple_of((me_lon % 2) * 128, 128), 128), :] = departed[me_lon]
+
+    def accumulate(step, carry):
+        chip = lax.rem(me_chip + near_first(step, chips), chips)
         for core in range(2):
             source = chip * 2 + core
 
@@ -201,9 +249,6 @@
             def _():
                 row_copy(source, 0, source, source).wait_recv()
 
-    def accumulate(step, carry):
-        chip = lax.rem(me_lon // 2 + ring_offset(step, chips), chips)
-        gather_chip(chip)
         for part in range(3):
             here = slice(part * (KF // 3), (part + 1) * (KF // 3))
             total[here, :] += jnp.dot(table[chip, here, :], sectors[chip], preferred_element_type=jnp.float32)
@@ -224,15 +269,21 @@
     blocks[...] = total[...].astype(jnp.bfloat16).reshape(blocks.shape)
 
     def send_blocks(step, carry):
-        block = lax.rem(me_lon + step, lon)
-        block_copy(me_lon, block, block, me_lon).start()
-        return carry
-
-    lax.fori_loop(1, lon, send_blocks, 0)
+        chip = lax.rem(me_chip + far_first(step, chips), chips)
+        for core in range(2):
+            block = chip * 2 + core
+
+            @pl.when(block != me_lon)
+            def _():
+                block_copy(me_lon, block, block, me_lon).start()
+
+        return carry
+
+    lax.fori_loop(0, chips, send_blocks, 0)
     wide[pl.ds(pl.multiple_of(me_lon * depth, depth), depth), :] = blocks[me_lon].astype(jnp.float32)
 
     def widen(step, carry):
-        chip = lax.rem(me_lon // 2 + ring_offset(step, chips), chips)
+        chip = lax.rem(me_chip + near_first(step, chips), chips)
         for core in range(2):
             source = chip * 2 + core
 
@@ -256,7 +307,8 @@
         )
 
     def send_bands(step, carry):
-        target = lax.rem(me_lat + step, lat)
+        column = lax.rem(me_lat % flat + far_first(step // tall, flat), flat)
+        target = lax.rem(me_lat // flat + far_first(step % tall, tall), tall) * flat + column
         picked = [wide[pl.ds(target * each + k, lon, stride=depth), :] for k in range(each)]
         packs[target] = jnp.concatenate(picked, axis=0).astype(jnp.bfloat16)
 
@@ -266,8 +318,11 @@
 
         return carry
 
-    lax.fori_loop(1, lat + 1, send_bands, 0)
+    lax.fori_loop(0, lat, send_bands, 0)
     bands[me_lat] = packs[me_lat]
+
+    for side in range(2):
+        tile_copy(side).wait_send()
 
     def finish_rows(step, carry):
         peer = lax.rem(me_lon + step, lon)
@@ -287,16 +342,21 @@
     out_ref[...] = bands[...]
 
 
-def transform(lon, lat, ends, cells, left, own, right):
+def transform(lon, lat, count, cells, own):
     vmem = pl.BlockSpec(memory_space=pltpu.VMEM)
     depth = KF // lon
     band = (lat, depth // lat * lon, 128)
+    small = small_tables()
     return pl.pallas_call(
         functools.partial(transform_kernel, lon, lat),
         out_shape=jax.ShapeDtypeStruct(band, jnp.bfloat16),
-        in_specs=[pl.BlockSpec(memory_space=pltpu.SMEM)] + [vmem] * 10,
+        in_specs=[pl.BlockSpec(memory_space=pltpu.HBM)] * 4,
         out_specs=vmem,
         scratch_shapes=[
+            pltpu.SMEM((3,), jnp.int32),
+            pltpu.VMEM((COLS // 128, 128), jnp.int32),
+            pltpu.VMEM((COLS, 128), jnp.bfloat16),
+            pltpu.VMEM(small.shape, jnp.float32),
             pltpu.VMEM((3 * BLOCKS, BLK * 128), jnp.bfloat16),
             pltpu.VMEM((COLS, 2 * BLOCKS), jnp.bfloat16),
             pltpu.VMEM((COLS, 128), jnp.float32),
@@ -311,6 +371,9 @@
             pltpu.VMEM((lon * depth, 128), jnp.float32),
             pltpu.VMEM(band, jnp.bfloat16),
             pltpu.VMEM(band, jnp.bfloat16),
+            pltpu.SemaphoreType.DMA((4,)),
+            pltpu.SemaphoreType.DMA((2,)),
+            pltpu.SemaphoreType.DMA((2,)),
             pltpu.SemaphoreType.DMA((lon,)),
             pltpu.SemaphoreType.DMA((lon,)),
             pltpu.SemaphoreType.DMA((lon,)),
@@ -319,20 +382,18 @@
             pltpu.SemaphoreType.DMA((lat,)),
         ],
         compiler_params=pltpu.CompilerParams(
-            vmem_limit_bytes=48 << 20, collective_id=0, has_side_effects=True
+            vmem_limit_bytes=62976 << 10, collective_id=0, has_side_effects=True
         ),
         name="transform",
-    )(ends, cells, left, own, right, *small_tables())
+    )(count, cells, own, small)
 
 
 def gathered_bands(fields, req_block, req_stencil, req_frac, req_count):
     lon = lax.axis_size("lon")
     lat = lax.axis_size("lat")
-    tile = fields.reshape(BLOCKS, BLK * 128)
-    left = lax.ppermute(tile, "lon", [(i, (i + 1) % lon) for i in range(lon)])
-    right = lax.ppermute(tile, "lon", [((i + 1) % lon, i) for i in range(lon)])
-    cells, ends = cell_requests(req_block[0, 0], req_stencil[0, 0], req_frac[0, 0], req_count[0, 0])
-    bands = transform(lon, lat, ends, cells, left, tile, right)
+    count = req_count[0, 0]
+    cells = order_requests(count, req_block[0, 0], req_stencil[0, 0], req_frac[0, 0])
+    bands = transform(lon, lat, count, cells, fields.reshape(COLS, 128))
     own = KF // lon // lat
     bands = bands.reshape(lat, own, lon, 128).transpose(1, 0, 2, 3)
     return bands.reshape(own, lat * lon, 128)

time: 111 us -> 96.6 us (0.87)
  starting transfers between devices: 10.5 us -> 0 us
  Pallas kernels: 84.4 us -> 91.8 us
  local copies, waits for them, and re-layouts: 10.8 us -> 3.67 us
  between operations: 2.94 us -> 0.03 us
  other arithmetic: 1.38 us -> 0.01 us
    ppermute x2 -> x0, starting transfers between devices: 10.5 us -> none  [the longest x1 7.04 us: gathered_bands(): right = lax.ppermute(tile, 'lon', [((i + 1) % lon, i) for i in range(lon)])]
    pallas_call x1, Pallas kernels: 84.4 us -> 90.2 us  [transform(): pl.pallas_call(functools.partial(transform_kernel, lon, lat), out_shape=j...]
    unnamed x15 -> x3, local copies, waits for them, and re-layouts: 5.23 us -> 1.48 us
    slice x4 -> x0, local copies, waits for them, and re-layouts: 2.21 us -> none  [the longest x1 1.31 us: cell_requests(): second = first + counts[1]]
    pallas_call x0 -> x1, Pallas kernels: none -> 1.58 us  [order_requests(): pl.pallas_call(order_kernel, out_shape=jax.ShapeDtypeStruct((COLS // 128,...]
    reshape x1 -> x0, local copies, waits for them, and re-layouts: 1.57 us -> none  [gathered_bands(): tile = fields.reshape(BLOCKS, BLK * 128)]
  transfers between devices with their start and end apart: 2 -> 0, of which waited for: 0 -> 0; matrix products, arithmetic and copies ran while one was open for 5% -> 0% of each run, Pallas kernels for 0% -> 0%
where the time goes in v3:
time: 96.6 us; the launch traced here: 96 us
  Pallas kernels  91.8 us (95%)
  local copies, waits for them, and re-layouts  3.67 us (4%)
    pallas_call x1, Pallas kernels, transform(): pl.pallas_call(functools.partial(transform_kernel, lon, lat), out_shape=j...  90.2 us

profile of v3, /device:TPU:1, one launch (start us, length us, event | category | flops | bytes accessed | tf_op | source)
XLA Modules:
  0.0 96.0 jit_solution(15396422678151906721)
XLA Ops:
  0.0 0.0 copy-start
  0.0 1.5 %copy.16 = s32[1,1,3,1280]{3,2,1,0:T(4,128)} copy(s32[1,1,3,1280]{3,1,2,0:T(1,128)} %param.8) | data formatting | bytes 30720
  1.5 1.6 %order_requests.1.cells_hbm = s32[24,128]{1,0:T(8,128)} custom-call(s32[3]{0:T(128)} %bitcast.21, s32[3,1280]{1,0:T(4,128)} %bitcast.18, s32[3,4,1280]{2,1,0:T(4,128)} %bitcast.19, s32[3,2,1280]{2,1,0:T(2,128)} %bitcast.20), custom_call_target="tpu_custom_call" | custom-call | tf_op jit(solution)/shard_map/order_requests/pallas_call | solution.py:68
  3.1 90.2 %transform.1 = bf16[32,48,128]{2,1,0:T(8,128)(2,1)} custom-call(s32[3]{0:T(128)} %bitcast.22, s32[24,128]{1,0:T(8,128)} %order_requests.1.cells_hbm, bf16[3072,128]{1,0:T(8,128)(2,1)} %bitcast.17, f32[256,128]{1,0:T(8,128)} %constant.9.clone.table_ref), custom_call_target="tpu_custom_call" | custom-call | tf_op jit(solution)/shard_map/transform/pallas_call | solution.py:350
  93.3 1.0 %copy.10 = bf16[32,2,24,128]{3,2,0,1:T(8,128)(2,1)S(1)} copy(bf16[32,2,24,128]{3,2,1,0:T(8,128)(2,1)} %bitcast.15) | data formatting | bytes 786432 | tf_op jit(solution)/shard_map/reshape | solution.py:398
  94.3 0.0 copy-done
  94.3 0.5 fusion
  94.9 1.1 %copy.12 = f32[2,768,128]{2,1,0:T(8,128)} copy(f32[2,768,128]{1,2,0:T(8,128)S(1)} %fusion) | data formatting | bytes 1572864 | tf_op jit(solution)/shard_map/mul | solution.py:407
  (1 shorter events, 0.0 us)
Async XLA Ops:
  0.0 94.3 %copy-start = (bf16[2,768,768]{2,1,0:T(8,128)(2,1)S(1)}, bf16[2,768,768]{2,1,0:T(8,128)(2,1)}, u32[]{:S(2)}) copy-start(bf16[2,768,768]{2,1,0:T(8,128)(2,1)} %param.12) | copy-start | bytes 7077892

commit v4 on v3

v4 whole, which is shorter than its diff:
```python
import functools
import math

import jax
import jax.numpy as jnp
import numpy as np
from jax import lax
from jax.experimental import pallas as pl
from jax.experimental.pallas import tpu as pltpu
from jax.sharding import PartitionSpec as P

KF = 1536
NN = 768
BLK = 16
FRAC = 16
COLS = 3072
CAP = 1280
NLON = 3072
BLOCKS = COLS // BLK
FINE = 96
CHUNK = 4
MESH = pl.DeviceIdType.MESH


def small_tables():
    unit = 2.0 * math.pi / NLON
    fine = np.concatenate([np.arange(0, FINE, 2), np.arange(1, FINE, 2)]).astype(np.int64)[:, None]
    lane = np.arange(128, dtype=np.int64)[None, :]
    scale = 1.0 / math.sqrt(NLON)
    near = unit * (fine * lane % NLON)
    plus = (np.cos(near) + np.sin(near)) * scale
    minus = (np.cos(near) - np.sin(near)) * scale
    far = unit * (fine * lane * 128 % NLON)
    coarse = unit * (np.arange(KF // FINE, dtype=np.int64)[:, None] * FINE * lane % NLON)
    tables = [plus, minus, np.cos(far), np.sin(far), np.cos(coarse), np.sin(coarse)]
    return np.concatenate(tables, axis=0).astype(np.float32)


def order_requests(first, second, block_ref, stencil_ref, frac_ref, cells_ref):
    lane = lax.broadcasted_iota(jnp.int32, (32, 128), 1)
    cell = lax.broadcasted_iota(jnp.int32, (32, 128), 0) * 128 + lane
    shift4 = 20 - 4 * lax.broadcasted_iota(jnp.int32, (4, CAP), 0)
    shift2 = 4 - 4 * lax.broadcasted_iota(jnp.int32, (2, CAP), 0)
    result = None
    for slot, start in ((0, None), (1, first), (2, second)):
        word = (
            lax.shift_left(block_ref[slot], jnp.full((1, CAP), 24, jnp.int32))
            + jnp.sum(lax.shift_left(stencil_ref[slot], shift4), axis=0, keepdims=True)
            + jnp.sum(lax.shift_left(frac_ref[slot], shift2), axis=0, keepdims=True)
        )
        pieces = [word[:, k * 128 : (k + 1) * 128] for k in range(CAP // 128)]
        pieces.append(jnp.zeros((32 - CAP // 128, 128), jnp.int32))
        placed = jnp.concatenate(pieces, axis=0)
        if start is None:
            result = placed
            continue
        moved = jnp.full((32, 128), start, jnp.int32)
        for bit in range(12):
            if bit < 7:
                turned = pltpu.roll(placed, 1 << bit, 1)
                turned = jnp.where(lane < (1 << bit), pltpu.roll(turned, 1, 0), turned)
            else:
                turned = pltpu.roll(placed, 1 << (bit - 7), 0)
            chosen = lax.shift_right_logical(moved, jnp.full((32, 128), bit, jnp.int32)) & 1
            placed = jnp.where(chosen == 1, turned, placed)
        result = jnp.where(cell < moved, result, placed)
    cells_ref[...] = result[: cells_ref.shape[0], :]


def decode(first, second, cells_ref, onehot_ref, weight_ref):
    rows = cells_ref.shape[0]
    columns = jnp.concatenate(
        [cells_ref[...], jnp.zeros((128 - rows, 128), jnp.int32)], axis=0
    ).T
    lane = lax.broadcasted_iota(jnp.int32, (128, 128), 1)
    sub = lax.broadcasted_iota(jnp.int32, (128, 128), 0)
    for row in range(rows):
        word = jnp.broadcast_to(columns[:, row : row + 1], (128, 128))
        block = lax.shift_right_logical(word, 24)
        edge = first if row < rows // 2 else second
        block = block + jnp.where(sub + row * 128 >= edge, BLOCKS, 0)
        here = pl.ds(row * 128, 128)
        for part in range(3):
            onehot_ref[here, part * 128 : (part + 1) * 128] = jnp.where(
                block == lane + part * 128, 1.0, 0.0
            ).astype(jnp.bfloat16)
        frac_lat = ((lax.shift_right_logical(word, 4) & 15).astype(jnp.float32) + 0.5) / FRAC
        frac_lon = ((word & 15).astype(jnp.float32) + 0.5) / FRAC
        corner = (
            (1.0 - frac_lat) * (1.0 - frac_lon),
            frac_lat * (1.0 - frac_lon),
            (1.0 - frac_lat) * frac_lon,
            frac_lat * frac_lon,
        )
        weight = jnp.zeros((128, 128), jnp.float32)
        for k in range(4):
            spot = lax.shift_right_logical(word, 20 - 4 * k) & 15
            weight = weight + jnp.where(spot == lane, corner[k], 0.0)
        weight_ref[here, :] = weight


def fill_table(small, plus, minus, table):
    near_plus, near_minus, far_cos, far_sin = [small.at[pl.ds(k * FINE, FINE)] for k in range(4)]
    coarse_cos, coarse_sin = [small.at[pl.ds(4 * FINE + k * (KF // FINE), KF // FINE)] for k in range(2)]
    for sector in range(NLON // 128):
        here = pl.ds(sector * 128, 128)
        turn_cos = far_cos[:, sector : sector + 1]
        turn_sin = far_sin[:, sector : sector + 1]
        plus[:, here] = turn_cos * near_plus[...] + turn_sin * near_minus[...]
        minus[:, here] = turn_cos * near_minus[...] - turn_sin * near_plus[...]

    def body(step, carry):
        cos = coarse_cos[pl.ds(step, 1), :]
        sin = coarse_sin[pl.ds(step, 1), :]
        for parity in range(2):
            here = slice(parity * (FINE // 2), (parity + 1) * (FINE // 2))
            rows = pl.ds(pl.multiple_of(step * (FINE // 2), FINE // 2) + parity * (KF // 2), FINE // 2)
            for sector in range(NLON // 128):
                lanes = slice(sector * 128, (sector + 1) * 128)
                table[sector // 2, rows, (sector % 2) * 128 : (sector % 2 + 1) * 128] = (
                    cos * plus[here, lanes] + sin * minus[here, lanes]
                ).astype(jnp.bfloat16)
        return carry

    lax.fori_loop(0, KF // FINE, body, 0)


def near_first(step, count):
    return jnp.where(step % 2 == 1, (step + 1) // 2, count - step // 2)


def far_first(step, count):
    away = count // 2 - (step + 1) // 2
    return jnp.where(step % 2 == 1, away, count - away)


def transform_kernel(lon, lat, count_hbm, block_hbm, stencil_hbm, frac_hbm, own_hbm, table_hbm, out_ref, *refs):
    (count_ref, block_ref, stencil_ref, frac_ref, own_ref, small) = refs[:6]
    (cells_ref, tiles, onehot, weight, departed, sectors, detour, plus, minus, table, total) = refs[6:17]
    (blocks, landed, bypass, wide, packs, bands) = refs[17:23]
    (fetch_sem, send_tile, recv_tile, send_row, recv_row, detour_sem, onward_row) = refs[23:30]
    (send_block, recv_block, bypass_sem, onward_block, send_band, recv_band) = refs[30:]
    me_lon, me_lat = lax.axis_index("lon"), lax.axis_index("lat")
    rows = departed.shape[0]
    depth = blocks.shape[2]
    each = depth // lat
    chips = lon // 2
    me_chip, me_core = me_lon // 2, me_lon % 2
    tall = 8 if lat == 32 else lat
    flat = lat // tall
    quarter = (chips // 4, chips - chips // 4)

    barrier = pltpu.get_barrier_semaphore()

    def greet_lon(step, carry):
        peer = lax.rem(me_lon + step, lon)
        pl.semaphore_signal(barrier, inc=1, device_id={"lon": peer}, device_id_type=MESH)
        return carry

    def greet_lat(step, carry):
        peer = lax.rem(me_lat + step, lat)
        pl.semaphore_signal(barrier, inc=1, device_id={"lat": peer}, device_id_type=MESH)
        return carry

    lax.fori_loop(1, lon, greet_lon, 0)
    lax.fori_loop(1, lat, greet_lat, 0)
    pairs = (
        (own_hbm, own_ref),
        (count_hbm, count_ref),
        (block_hbm, block_ref),
        (stencil_hbm, stencil_ref),
        (frac_hbm, frac_ref),
        (table_hbm, small),
    )
    fetches = [pltpu.make_async_copy(src, dst, fetch_sem.at[k]) for k, (src, dst) in enumerate(pairs)]
    for fetch in fetches:
        fetch.start()
    fetches[0].wait()

    weight[...] = own_ref[...].astype(jnp.float32)
    for cell in range(BLK):
        tiles[BLOCKS : 2 * BLOCKS, cell * 128 : (cell + 1) * 128] = weight[
            pl.ds(cell, BLOCKS, stride=BLK), :
        ].astype(jnp.bfloat16)
    pl.semaphore_wait(barrier, lon + lat - 2)

    def tile_copy(side):
        return pltpu.make_async_remote_copy(
            src_ref=tiles.at[pl.ds(BLOCKS, BLOCKS)],
            dst_ref=tiles.at[pl.ds(2 * BLOCKS * side, BLOCKS)],
            send_sem=send_tile.at[side],
            recv_sem=recv_tile.at[side],
            device_id={"lon": lax.rem(me_lon + jnp.where(side == 0, 1, lon - 1), lon)},
            device_id_type=MESH,
        )

    tile_copy(me_core).start()
    tile_copy(1 - me_core).start()
    for fetch in fetches[1:]:
        fetch.wait()
    first = count_ref[0]
    second = first + count_ref[1]
    order_requests(first, second, block_ref, stencil_ref, frac_ref, cells_ref)
    decode(first, second, cells_ref, onehot, weight)

    def slot_of(source):
        return sectors.at[source // 2, pl.ds(pl.multiple_of((source % 2) * 128, 128), 128), :]

    def row_copy(source, row, slot_send, slot_recv):
        return pltpu.make_async_remote_copy(
            src_ref=departed.at[row],
            dst_ref=slot_of(source),
            send_sem=send_row.at[slot_send],
            recv_sem=recv_row.at[slot_recv],
            device_id={"lon": row},
            device_id_type=MESH,
        )

    def row_detour(row, core):
        return pltpu.make_async_remote_copy(
            src_ref=departed.at[row],
            dst_ref=detour.at[core],
            send_sem=send_row.at[row],
            recv_sem=detour_sem.at[core],
            device_id={"lon": lax.rem(me_chip + quarter[core], chips) * 2 + me_core},
            device_id_type=MESH,
        )

    def row_onward(core):
        source = lax.rem(me_chip + chips - quarter[core], chips) * 2 + me_core
        return pltpu.make_async_remote_copy(
            src_ref=detour.at[core],
            dst_ref=slot_of(source),
            send_sem=onward_row.at[core],
            recv_sem=recv_row.at[source],
            device_id={"lon": lax.rem(me_chip + quarter[core], chips) * 2 + core},
            device_id_type=MESH,
        )

    parts = rows // CHUNK

    def interpolate(part, carry):
        low = pl.multiple_of(jnp.where(part < parts // 2, 0, BLOCKS), BLOCKS)
        here = pl.ds(pl.multiple_of(part * CHUNK * 128, CHUNK * 128), CHUNK * 128)
        values = jnp.zeros((CHUNK * 128, 128), jnp.float32)
        for pair in range(BLK // 2):
            got = jnp.dot(
                onehot[here, :],
                tiles[pl.ds(low, 2 * BLOCKS), pair * 256 : (pair + 1) * 256],
                preferred_element_type=jnp.float32,
            )
            scale = weight[here, :]
            values = values + scale[:, 2 * pair : 2 * pair + 1] * got[:, :128]
            values = values + scale[:, 2 * pair + 1 : 2 * pair + 2] * got[:, 128:]
        departed[pl.ds(part * CHUNK, CHUNK)] = values.astype(jnp.bfloat16).reshape(CHUNK, 128, 128)

        def send_rows(pair, inner):
            chip = part * (CHUNK // 2) + pair
            opposite = lax.rem(chip + chips - me_chip, chips) == chips // 2
            for core in range(2):
                row = chip * 2 + core

                @pl.when(opposite)
                def _():
                    row_detour(row, core).start()

                @pl.when(jnp.logical_and(jnp.logical_not(opposite), row != me_lon))
                def _():
                    row_copy(me_lon, row, row, me_lon).start()

            return inner

        lax.fori_loop(0, CHUNK // 2, send_rows, 0)
        return carry

    for turn in range(2):
        half = 1 - me_core if turn == 0 else me_core
        tile_copy(half).wait_recv()
        lax.fori_loop(half * (parts // 2), (half + 1) * (parts // 2), interpolate, 0)
    slot_of(me_lon)[...] = departed[me_lon]
    fill_table(small, plus, minus, table)
    total[...] = jnp.zeros_like(total)
    for core in range(2):
        row_detour(0, core).wait_recv()
        row_onward(core).start()

    def accumulate(step, carry):
        chip = lax.rem(me_chip + near_first(step, chips), chips)
        for core in range(2):
            source = chip * 2 + core

            @pl.when(source != me_lon)
            def _():
                row_copy(source, 0, source, source).wait_recv()

        for part in range(3):
            here = slice(part * (KF // 3), (part + 1) * (KF // 3))
            total[here, :] += jnp.dot(table[chip, here, :], sectors[chip], preferred_element_type=jnp.float32)
        return carry

    lax.fori_loop(0, chips, accumulate, 0)

    def block_copy(parity, source, block, slot_send, slot_recv):
        return pltpu.make_async_remote_copy(
            src_ref=blocks.at[parity, block],
            dst_ref=landed.at[parity, source],
            send_sem=send_block.at[parity, slot_send],
            recv_sem=recv_block.at[parity, slot_recv],
            device_id={"lon": block},
            device_id_type=MESH,
        )

    def block_detour(parity, core):
        block = lax.rem(me_chip + chips // 2, chips) * 2 + core
        return pltpu.make_async_remote_copy(
            src_ref=blocks.at[parity, block],
            dst_ref=bypass.at[parity, core],
            send_sem=send_block.at[parity, block],
            recv_sem=bypass_sem.at[parity, core],
            device_id={"lon": lax.rem(me_chip + quarter[core], chips) * 2 + me_core},
            device_id_type=MESH,
        )

    def block_onward(parity, core):
        source = lax.rem(me_chip + chips - quarter[core], chips) * 2 + me_core
        return pltpu.make_async_remote_copy(
            src_ref=bypass.at[parity, core],
            dst_ref=landed.at[parity, source],
            send_sem=onward_block.at[parity, core],
            recv_sem=recv_block.at[parity, source],
            device_id={"lon": lax.rem(me_chip + quarter[core], chips) * 2 + core},
            device_id_type=MESH,
        )

    blocks[...] = total[...].astype(jnp.bfloat16).reshape(blocks.shape)
    for parity in range(2):
        for core in range(2):
            block_detour(parity, core).start()
    for parity in range(2):

        def send_blocks(step, carry):
            chip = lax.rem(me_chip + far_first(step, chips), chips)
            for core in range(2):
                block = chip * 2 + core

                @pl.when(block != me_lon)
                def _():
                    block_copy(parity, me_lon, block, block, me_lon).start()

            return carry

        lax.fori_loop(1, chips, send_blocks, 0)
    for parity in range(2):
        for core in range(2):
            block_detour(parity, core).wait_recv()
            block_onward(parity, core).start()

    def band_copy(parity, source, target, slot_send, slot_recv):
        return pltpu.make_async_remote_copy(
            src_ref=packs.at[parity, target],
            dst_ref=bands.at[parity, source],
            send_sem=send_band.at[parity, slot_send],
            recv_sem=recv_band.at[parity, slot_recv],
            device_id={"lat": target},
            device_id_type=MESH,
        )

    for parity in range(2):
        wide[parity, pl.ds(pl.multiple_of(me_lon * depth, depth), depth), :] = blocks[parity, me_lon].astype(jnp.float32)

        def widen(step, carry):
            chip = lax.rem(me_chip + near_first(step, chips), chips)
            for core in range(2):
                source = chip * 2 + core

                @pl.when(source != me_lon)
                def _():
                    block_copy(parity, source, 0, source, source).wait_recv()
                    here = pl.ds(pl.multiple_of(source * depth, depth), depth)
                    wide[parity, here, :] = landed[parity, source].astype(jnp.float32)

            return carry

        lax.fori_loop(0, chips, widen, 0)

        def send_bands(step, carry):
            column = lax.rem(me_lat % flat + far_first(step // tall, flat), flat)
            target = lax.rem(me_lat // flat + far_first(step % tall, tall), tall) * flat + column
            picked = [wide[parity, pl.ds(target * each + k, lon, stride=depth), :] for k in range(each)]
            packs[parity, target] = jnp.concatenate(picked, axis=0).astype(jnp.bfloat16)

            @pl.when(target != me_lat)
            def _():
                band_copy(parity, me_lat, target, target, me_lat).start()

            return carry

        lax.fori_loop(0, lat, send_bands, 0)
        bands[parity, me_lat] = packs[parity, me_lat]

    for side in range(2):
        tile_copy(side).wait_send()
        row_onward(side).wait_send()

    def finish_rows(step, carry):
        peer = lax.rem(me_lon + step, lon)
        row_copy(me_lon, peer, peer, me_lon).wait_send()
        for parity in range(2):
            block_copy(parity, me_lon, peer, peer, me_lon).wait_send()
        return carry

    lax.fori_loop(1, lon, finish_rows, 0)
    for parity in range(2):
        for core in range(2):
            block_onward(parity, core).wait_send()

    def finish_bands(step, carry):
        peer = lax.rem(me_lat + step, lat)
        for parity in range(2):
            band_copy(parity, peer, 0, peer, peer).wait_recv()
            band_copy(parity, me_lat, peer, peer, me_lat).wait_send()
        return carry

    lax.fori_loop(1, lat, finish_bands, 0)
    out_ref[...] = bands[...]


def transform(lon, lat, count, block, stencil, frac, own):
    depth = KF // lon // 2
    band = (2, lat, depth // lat * lon, 128)
    small = small_tables()
    return pl.pallas_call(
        functools.partial(transform_kernel, lon, lat),
        out_shape=jax.ShapeDtypeStruct(band, jnp.bfloat16),
        in_specs=[pl.BlockSpec(memory_space=pltpu.HBM)] * 6,
        out_specs=pl.BlockSpec(memory_space=pltpu.VMEM),
        scratch_shapes=[
            pltpu.SMEM((3,), jnp.int32),
            pltpu.VMEM(block.shape, jnp.int32),
            pltpu.VMEM(stencil.shape, jnp.int32),
            pltpu.VMEM(frac.shape, jnp.int32),
            pltpu.VMEM((COLS, 128), jnp.bfloat16),
            pltpu.VMEM(small.shape, jnp.float32),
            pltpu.VMEM((COLS // 128, 128), jnp.int32),
            pltpu.VMEM((3 * BLOCKS, BLK * 128), jnp.bfloat16),
            pltpu.VMEM((COLS, 2 * BLOCKS), jnp.bfloat16),
            pltpu.VMEM((COLS, 128), jnp.float32),
            pltpu.VMEM((COLS // 128, 128, 128), jnp.bfloat16),
            pltpu.VMEM((lon // 2, 256, 128), jnp.bfloat16),
            pltpu.VMEM((2, 128, 128), jnp.bfloat16),
            pltpu.VMEM((FINE, NLON), jnp.float32),
            pltpu.VMEM((FINE, NLON), jnp.float32),
            pltpu.VMEM((NLON // 256, KF, 256), jnp.bfloat16),
            pltpu.VMEM((KF, 128), jnp.float32),
            pltpu.VMEM((2, lon, depth, 128), jnp.bfloat16),
            pltpu.VMEM((2, lon, depth, 128), jnp.bfloat16),
            pltpu.VMEM((2, 2, depth, 128), jnp.bfloat16),
            pltpu.VMEM((2, lon * depth, 128), jnp.float32),
            pltpu.VMEM(band, jnp.bfloat16),
            pltpu.VMEM(band, jnp.bfloat16),
            pltpu.SemaphoreType.DMA((6,)),
            pltpu.SemaphoreType.DMA((2,)),
            pltpu.SemaphoreType.DMA((2,)),
            pltpu.SemaphoreType.DMA((lon,)),
            pltpu.SemaphoreType.DMA((lon,)),
            pltpu.SemaphoreType.DMA((2,)),
            pltpu.SemaphoreType.DMA((2,)),
            pltpu.SemaphoreType.DMA((2, lon)),
            pltpu.SemaphoreType.DMA((2, lon)),
            pltpu.SemaphoreType.DMA((2, 2)),
            pltpu.SemaphoreType.DMA((2, 2)),
            pltpu.SemaphoreType.DMA((2, lat)),
            pltpu.SemaphoreType.DMA((2, lat)),
        ],
        compiler_params=pltpu.CompilerParams(
            vmem_limit_bytes=62976 << 10, collective_id=0, has_side_effects=True
        ),
        name="transform",
    )(count, block, stencil, frac, own, small)


def gathered_bands(fields, req_block, req_stencil, req_frac, req_count):
    lon = lax.axis_size("lon")
    lat = lax.axis_size("lat")
    block = req_block[0, 0].reshape(3, 1, CAP)
    bands = transform(
        lon, lat, req_count[0, 0], block, req_stencil[0, 0], req_frac[0, 0], fields.reshape(COLS, 128)
    )
    half = KF // lon // lat // 2
    bands = bands.reshape(2, lat, half, lon, 128).transpose(2, 0, 1, 3, 4)
    return bands.reshape(2 * half, lat * lon, 128)


def local(fields, req_block, req_stencil, req_frac, req_count, legendre):
    gathered = gathered_bands(fields, req_block, req_stencil, req_frac, req_count)
    projected = jnp.einsum("kyn,kyc->knc", legendre, gathered, preferred_element_type=jnp.float32)
    degree = jnp.arange(NN, dtype=jnp.float32)
    factor = 1.0 / (1.0 + 4.0 * degree * (degree + 1.0) / (NN * (NN + 1)))
    return projected * factor[None, :, None]


def solution(mesh):
    return jax.shard_map(
        local,
        mesh=mesh,
        in_specs=(
            P("lat", "lon", None),
            P("lat", "lon", None, None),
            P("lat", "lon", None, None, None),
            P("lat", "lon", None, None, None),
            P("lat", "lon", None),
            P(("lon", "lat"), None, None),
        ),
        out_specs=P(("lon", "lat"), None, None),
        check_vma=False,
    )
```

time: 96.6 us -> 92.2 us (0.954)
  the two profiles are of different devices: /device:TPU:1 before, /device:TPU:8 now
where the time goes in v4:
time: 92.2 us; the launch traced here: 92.1 us
  Pallas kernels  89.4 us (97%)
  matrix products  1.52 us (2%)
  local copies, waits for them, and re-layouts  1.15 us (1%)
    pallas_call x1, Pallas kernels, transform(): pl.pallas_call(functools.partial(transform_kernel, lon, lat), out_shape=j...  89.4 us

profile of v4, /device:TPU:8, one launch (start us, length us, event | category | flops | bytes accessed | tf_op | source)
XLA Modules:
  0.0 92.1 jit_solution(4778971279245672332)
XLA Ops:
  0.0 0.0 copy-start
  0.0 89.4 %transform.1 = bf16[2,32,24,128]{3,2,1,0:T(8,128)(2,1)} custom-call(s32[3]{0:T(128)} %bitcast.15, s32[3,1,1280]{2,1,0:T(1,128)} %bitcast.14, s32[3,4,1280]{2,1,0:T(4,128)} %bitcast.12, s32[3,2,1280]{2,1,0:T(2,128)} %bitcast.13, bf16[3072,128]{1,0:T(8,128)(2,1)} %bitcast.11, f32[416,128]{1,0:T(8,128)} %constant.9.clone.table_hbm), custom_call_target="tpu_custom_call" | custom-call | tf_op jit(solution)/shard_map/transform/pallas_call | solution.py:432
  89.4 0.0 copy-done
  89.4 1.5 %fusion = f32[2,768,128]{1,2,0:T(8,128)S(1)} fusion(bf16[2,768,128]{2,1,0:T(8,128)(2,1)} %bitcast.10, bf16[2,768,768]{2,1,0:T(8,128)(2,1)S(1)} %copy-done, f32[768]{0:T(1024)S(1)} %fusion.4), kind=kOutput, calls=%fused_computation.1 | convolution fusion | flops 302186496 | bytes 3542016 | tf_op jit(solution)/shard_map/kyn,kyc->knc/dot_general | solution.py:496
  90.9 1.1 %copy.9 = f32[2,768,128]{2,1,0:T(8,128)} copy(f32[2,768,128]{1,2,0:T(8,128)S(1)} %fusion) | data formatting | bytes 1572864 | tf_op jit(solution)/shard_map/mul | solution.py:499
  (1 shorter events, 0.0 us)
Async XLA Ops:
  0.0 89.4 %copy-start = (bf16[2,768,768]{2,1,0:T(8,128)(2,1)S(1)}, bf16[2,768,768]{2,1,0:T(8,128)(2,1)}, u32[]{:S(2)}) copy-start(bf16[2,768,768]{2,1,0:T(8,128)(2,1)} %param.12) | copy-start | bytes 7077892

commit v5 on v4

--- a/solution.py
+++ b/solution.py
@@ -19,6 +19,7 @@
 BLOCKS = COLS // BLK
 FINE = 96
 CHUNK = 4
+EDGE = CAP // 128
 MESH = pl.DeviceIdType.MESH
 
 
@@ -36,7 +37,7 @@
     return np.concatenate(tables, axis=0).astype(np.float32)
 
 
-def order_requests(first, second, block_ref, stencil_ref, frac_ref, cells_ref):
+def order_requests(first, second, block_ref, stencil_ref, frac_ref, outbox, cells_ref):
     lane = lax.broadcasted_iota(jnp.int32, (32, 128), 1)
     cell = lax.broadcasted_iota(jnp.int32, (32, 128), 0) * 128 + lane
     shift4 = 20 - 4 * lax.broadcasted_iota(jnp.int32, (4, CAP), 0)
@@ -64,23 +65,25 @@
             chosen = lax.shift_right_logical(moved, jnp.full((32, 128), bit, jnp.int32)) & 1
             placed = jnp.where(chosen == 1, turned, placed)
         result = jnp.where(cell < moved, result, placed)
-    cells_ref[...] = result[: cells_ref.shape[0], :]
-
-
-def decode(first, second, cells_ref, onehot_ref, weight_ref):
     rows = cells_ref.shape[0]
+    nobody = -(1 << 24)
+    outbox[0] = jnp.where(cell < first, result, result | nobody)[:rows, :]
+    late = jnp.where(cell >= second, result, result | nobody)
+    outbox[1] = pltpu.roll(late, 32 - rows + EDGE, 0)[:rows, :]
+    middle = jnp.where(jnp.logical_and(cell >= first, cell < second), result, result | nobody)
+    cells_ref[...] = middle[:rows, :]
+
+
+def decode(words, chosen, base, onehot_ref, weight_ref):
     columns = jnp.concatenate(
-        [cells_ref[...], jnp.zeros((128 - rows, 128), jnp.int32)], axis=0
+        [words, jnp.zeros((128 - words.shape[0], 128), jnp.int32)], axis=0
     ).T
     lane = lax.broadcasted_iota(jnp.int32, (128, 128), 1)
-    sub = lax.broadcasted_iota(jnp.int32, (128, 128), 0)
-    for row in range(rows):
+    for place, row in enumerate(chosen):
         word = jnp.broadcast_to(columns[:, row : row + 1], (128, 128))
         block = lax.shift_right_logical(word, 24)
-        edge = first if row < rows // 2 else second
-        block = block + jnp.where(sub + row * 128 >= edge, BLOCKS, 0)
-        here = pl.ds(row * 128, 128)
-        for part in range(3):
+        here = pl.ds(pl.multiple_of(base + place * 128, 128), 128)
+        for part in range(2):
             onehot_ref[here, part * 128 : (part + 1) * 128] = jnp.where(
                 block == lane + part * 128, 1.0, 0.0
             ).astype(jnp.bfloat16)
@@ -136,10 +139,10 @@
 
 def transform_kernel(lon, lat, count_hbm, block_hbm, stencil_hbm, frac_hbm, own_hbm, table_hbm, out_ref, *refs):
     (count_ref, block_ref, stencil_ref, frac_ref, own_ref, small) = refs[:6]
-    (cells_ref, tiles, onehot, weight, departed, sectors, detour, plus, minus, table, total) = refs[6:17]
-    (blocks, landed, bypass, wide, packs, bands) = refs[17:23]
-    (fetch_sem, send_tile, recv_tile, send_row, recv_row, detour_sem, onward_row) = refs[23:30]
-    (send_block, recv_block, bypass_sem, onward_block, send_band, recv_band) = refs[30:]
+    (outbox, inbox, give, take, cells_ref, tiles, onehot, weight, departed, sectors, detour, plus, minus, table, total) = refs[6:21]
+    (blocks, landed, wide, packs, bands) = refs[21:26]
+    (fetch_sem, send_word, recv_word, send_value, recv_value, send_row, recv_row, detour_sem, onward_row) = refs[26:35]
+    (send_block, recv_block, send_band, recv_band) = refs[35:]
     me_lon, me_lat = lax.axis_index("lon"), lax.axis_index("lat")
     rows = departed.shape[0]
     depth = blocks.shape[2]
@@ -177,31 +180,80 @@
         fetch.start()
     fetches[0].wait()
 
-    weight[...] = own_ref[...].astype(jnp.float32)
+    weight[:COLS, :] = own_ref[...].astype(jnp.float32)
     for cell in range(BLK):
-        tiles[BLOCKS : 2 * BLOCKS, cell * 128 : (cell + 1) * 128] = weight[
+        tiles[:BLOCKS, cell * 128 : (cell + 1) * 128] = weight[
             pl.ds(cell, BLOCKS, stride=BLK), :
         ].astype(jnp.bfloat16)
-    pl.semaphore_wait(barrier, lon + lat - 2)
-
-    def tile_copy(side):
-        return pltpu.make_async_remote_copy(
-            src_ref=tiles.at[pl.ds(BLOCKS, BLOCKS)],
-            dst_ref=tiles.at[pl.ds(2 * BLOCKS * side, BLOCKS)],
-            send_sem=send_tile.at[side],
-            recv_sem=recv_tile.at[side],
-            device_id={"lon": lax.rem(me_lon + jnp.where(side == 0, 1, lon - 1), lon)},
-            device_id_type=MESH,
-        )
-
-    tile_copy(me_core).start()
-    tile_copy(1 - me_core).start()
+    tiles[BLOCKS:, :] = jnp.zeros((256 - BLOCKS, BLK * 128), jnp.bfloat16)
     for fetch in fetches[1:]:
         fetch.wait()
     first = count_ref[0]
     second = first + count_ref[1]
-    order_requests(first, second, block_ref, stencil_ref, frac_ref, cells_ref)
-    decode(first, second, cells_ref, onehot, weight)
+    order_requests(first, second, block_ref, stencil_ref, frac_ref, outbox, cells_ref)
+    pl.semaphore_wait(barrier, lon + lat - 2)
+
+    def beside(side):
+        return lax.rem(me_lon + jnp.where(side == 0, lon - 1, 1), lon)
+
+    def word_copy(side):
+        return pltpu.make_async_remote_copy(
+            src_ref=outbox.at[side],
+            dst_ref=inbox.at[1 - side],
+            send_sem=send_word.at[side],
+            recv_sem=recv_word.at[1 - side],
+            device_id={"lon": beside(side)},
+            device_id_type=MESH,
+        )
+
+    def value_copy(side, piece):
+        here = pl.ds(piece * (EDGE // 2), EDGE // 2)
+        return pltpu.make_async_remote_copy(
+            src_ref=give.at[side, here],
+            dst_ref=take.at[1 - side, here],
+            send_sem=send_value.at[side, piece],
+            recv_sem=recv_value.at[1 - side, piece],
+            device_id={"lon": beside(side)},
+            device_id_type=MESH,
+        )
+
+    def weighted(base, count):
+        here = pl.ds(pl.multiple_of(base, 128), count)
+        values = jnp.zeros((count, 128), jnp.float32)
+        for pair in range(BLK // 2):
+            got = jnp.dot(
+                onehot[here, :],
+                tiles[:, pair * 256 : (pair + 1) * 256],
+                preferred_element_type=jnp.float32,
+            )
+            scale = weight[here, :]
+            values = values + scale[:, 2 * pair : 2 * pair + 1] * got[:, :128]
+            values = values + scale[:, 2 * pair + 1 : 2 * pair + 2] * got[:, 128:]
+        return values.astype(jnp.bfloat16).reshape(count // 128, 128, 128)
+
+    for side in range(2):
+        word_copy(side).start()
+    middle = range(4, 20)
+    decode(cells_ref[...], middle, 2 * CAP, onehot, weight)
+    for side in (me_core, 1 - me_core):
+        word_copy(1 - side).wait_recv()
+        decode(inbox[side], range(EDGE), side * CAP, onehot, weight)
+        for piece in range(2):
+            rows_here = pl.ds(piece * (EDGE // 2), EDGE // 2)
+            give[side, rows_here] = weighted(side * CAP + piece * (CAP // 2), CAP // 2)
+            value_copy(side, piece).start()
+    for piece in range(4):
+        departed[4 + piece * 4 : 8 + piece * 4] = weighted(2 * CAP + piece * 512, 512)
+    for side in range(2):
+        for piece in range(2):
+            value_copy(1 - side, piece).wait_recv()
+    departed[:4] = take[0, :4]
+    departed[20:] = take[1, 6:]
+    for low, side, start in ((4, 0, 4), (14, 1, 0)):
+        here = pl.ds(low, 6)
+        departed[here] = (
+            departed[here].astype(jnp.float32) + take[side, start : start + 6].astype(jnp.float32)
+        ).astype(jnp.bfloat16)
 
     def slot_of(source):
         return sectors.at[source // 2, pl.ds(pl.multiple_of((source % 2) * 128, 128), 128), :]
@@ -237,46 +289,22 @@
             device_id_type=MESH,
         )
 
-    parts = rows // CHUNK
-
-    def interpolate(part, carry):
-        low = pl.multiple_of(jnp.where(part < parts // 2, 0, BLOCKS), BLOCKS)
-        here = pl.ds(pl.multiple_of(part * CHUNK * 128, CHUNK * 128), CHUNK * 128)
-        values = jnp.zeros((CHUNK * 128, 128), jnp.float32)
-        for pair in range(BLK // 2):
-            got = jnp.dot(
-                onehot[here, :],
-                tiles[pl.ds(low, 2 * BLOCKS), pair * 256 : (pair + 1) * 256],
-                preferred_element_type=jnp.float32,
-            )
-            scale = weight[here, :]
-            values = values + scale[:, 2 * pair : 2 * pair + 1] * got[:, :128]
-            values = values + scale[:, 2 * pair + 1 : 2 * pair + 2] * got[:, 128:]
-        departed[pl.ds(part * CHUNK, CHUNK)] = values.astype(jnp.bfloat16).reshape(CHUNK, 128, 128)
-
-        def send_rows(pair, inner):
-            chip = part * (CHUNK // 2) + pair
-            opposite = lax.rem(chip + chips - me_chip, chips) == chips // 2
-            for core in range(2):
-                row = chip * 2 + core
-
-                @pl.when(opposite)
-                def _():
-                    row_detour(row, core).start()
-
-                @pl.when(jnp.logical_and(jnp.logical_not(opposite), row != me_lon))
-                def _():
-                    row_copy(me_lon, row, row, me_lon).start()
-
-            return inner
-
-        lax.fori_loop(0, CHUNK // 2, send_rows, 0)
-        return carry
-
-    for turn in range(2):
-        half = 1 - me_core if turn == 0 else me_core
-        tile_copy(half).wait_recv()
-        lax.fori_loop(half * (parts // 2), (half + 1) * (parts // 2), interpolate, 0)
+    def send_rows(step, carry):
+        chip = lax.rem(me_chip + far_first(step, chips), chips)
+        for core in range(2):
+            row = chip * 2 + core
+
+            @pl.when(step == 0)
+            def _():
+                row_detour(row, core).start()
+
+            @pl.when(jnp.logical_and(step > 0, row != me_lon))
+            def _():
+                row_copy(me_lon, row, row, me_lon).start()
+
+        return carry
+
+    lax.fori_loop(0, chips, send_rows, 0)
     slot_of(me_lon)[...] = departed[me_lon]
     fill_table(small, plus, minus, table)
     total[...] = jnp.zeros_like(total)
@@ -310,32 +338,7 @@
             device_id_type=MESH,
         )
 
-    def block_detour(parity, core):
-        block = lax.rem(me_chip + chips // 2, chips) * 2 + core
-        return pltpu.make_async_remote_copy(
-            src_ref=blocks.at[parity, block],
-            dst_ref=bypass.at[parity, core],
-            send_sem=send_block.at[parity, block],
-            recv_sem=bypass_sem.at[parity, core],
-            device_id={"lon": lax.rem(me_chip + quarter[core], chips) * 2 + me_core},
-            device_id_type=MESH,
-        )
-
-    def block_onward(parity, core):
-        source = lax.rem(me_chip + chips - quarter[core], chips) * 2 + me_core
-        return pltpu.make_async_remote_copy(
-            src_ref=bypass.at[parity, core],
-            dst_ref=landed.at[parity, source],
-            send_sem=onward_block.at[parity, core],
-            recv_sem=recv_block.at[parity, source],
-            device_id={"lon": lax.rem(me_chip + quarter[core], chips) * 2 + core},
-            device_id_type=MESH,
-        )
-
     blocks[...] = total[...].astype(jnp.bfloat16).reshape(blocks.shape)
-    for parity in range(2):
-        for core in range(2):
-            block_detour(parity, core).start()
     for parity in range(2):
 
         def send_blocks(step, carry):
@@ -349,11 +352,7 @@
 
             return carry
 
-        lax.fori_loop(1, chips, send_blocks, 0)
-    for parity in range(2):
-        for core in range(2):
-            block_detour(parity, core).wait_recv()
-            block_onward(parity, core).start()
+        lax.fori_loop(0, chips, send_blocks, 0)
 
     def band_copy(parity, source, target, slot_send, slot_recv):
         return pltpu.make_async_remote_copy(
@@ -399,7 +398,9 @@
         bands[parity, me_lat] = packs[parity, me_lat]
 
     for side in range(2):
-        tile_copy(side).wait_send()
+        word_copy(side).wait_send()
+        for piece in range(2):
+            value_copy(side, piece).wait_send()
         row_onward(side).wait_send()
 
     def finish_rows(step, carry):
@@ -410,9 +411,6 @@
         return carry
 
     lax.fori_loop(1, lon, finish_rows, 0)
-    for parity in range(2):
-        for core in range(2):
-            block_onward(parity, core).wait_send()
 
     def finish_bands(step, carry):
         peer = lax.rem(me_lat + step, lat)
@@ -441,10 +439,14 @@
             pltpu.VMEM(frac.shape, jnp.int32),
             pltpu.VMEM((COLS, 128), jnp.bfloat16),
             pltpu.VMEM(small.shape, jnp.float32),
+            pltpu.VMEM((2, COLS // 128, 128), jnp.int32),
+            pltpu.VMEM((2, COLS // 128, 128), jnp.int32),
+            pltpu.VMEM((2, EDGE, 128, 128), jnp.bfloat16),
+            pltpu.VMEM((2, EDGE, 128, 128), jnp.bfloat16),
             pltpu.VMEM((COLS // 128, 128), jnp.int32),
-            pltpu.VMEM((3 * BLOCKS, BLK * 128), jnp.bfloat16),
-            pltpu.VMEM((COLS, 2 * BLOCKS), jnp.bfloat16),
-            pltpu.VMEM((COLS, 128), jnp.float32),
+            pltpu.VMEM((256, BLK * 128), jnp.bfloat16),
+            pltpu.VMEM((2 * CAP + 2048, 256), jnp.bfloat16),
+            pltpu.VMEM((2 * CAP + 2048, 128), jnp.float32),
             pltpu.VMEM((COLS // 128, 128, 128), jnp.bfloat16),
             pltpu.VMEM((lon // 2, 256, 128), jnp.bfloat16),
             pltpu.VMEM((2, 128, 128), jnp.bfloat16),
@@ -454,21 +456,20 @@
             pltpu.VMEM((KF, 128), jnp.float32),
             pltpu.VMEM((2, lon, depth, 128), jnp.bfloat16),
             pltpu.VMEM((2, lon, depth, 128), jnp.bfloat16),
-            pltpu.VMEM((2, 2, depth, 128), jnp.bfloat16),
             pltpu.VMEM((2, lon * depth, 128), jnp.float32),
             pltpu.VMEM(band, jnp.bfloat16),
             pltpu.VMEM(band, jnp.bfloat16),
             pltpu.SemaphoreType.DMA((6,)),
             pltpu.SemaphoreType.DMA((2,)),
             pltpu.SemaphoreType.DMA((2,)),
+            pltpu.SemaphoreType.DMA((2, 2)),
+            pltpu.SemaphoreType.DMA((2, 2)),
             pltpu.SemaphoreType.DMA((lon,)),
             pltpu.SemaphoreType.DMA((lon,)),
             pltpu.SemaphoreType.DMA((2,)),
             pltpu.SemaphoreType.DMA((2,)),
             pltpu.SemaphoreType.DMA((2, lon)),
             pltpu.SemaphoreType.DMA((2, lon)),
-            pltpu.SemaphoreType.DMA((2, 2)),
-            pltpu.SemaphoreType.DMA((2, 2)),
             pltpu.SemaphoreType.DMA((2, lat)),
             pltpu.SemaphoreType.DMA((2, lat)),
         ],

time: 92.2 us -> 95.1 us (1.031)
  the two profiles are of different devices: /device:TPU:8 before, /device:TPU:1 now
where the time goes in v5:
time: 95.1 us; the launch traced here: 94.9 us
  Pallas kernels  92.2 us (97%)
  matrix products  1.52 us (2%)
  local copies, waits for them, and re-layouts  1.15 us (1%)
    pallas_call x1, Pallas kernels, transform(): pl.pallas_call(functools.partial(transform_kernel, lon, lat), out_shape=j...  92.2 us

profile of v5, /device:TPU:1, one launch (start us, length us, event | category | flops | bytes accessed | tf_op | source)
XLA Modules:
  0.0 94.9 jit_solution(11694337520368142555)
XLA Ops:
  0.0 0.0 copy-start
  0.0 92.2 %transform.1 = bf16[2,32,24,128]{3,2,1,0:T(8,128)(2,1)} custom-call(s32[3]{0:T(128)} %bitcast.15, s32[3,1,1280]{2,1,0:T(1,128)} %bitcast.14, s32[3,4,1280]{2,1,0:T(4,128)} %bitcast.12, s32[3,2,1280]{2,1,0:T(2,128)} %bitcast.13, bf16[3072,128]{1,0:T(8,128)(2,1)} %bitcast.11, f32[416,128]{1,0:T(8,128)} %constant.9.clone.table_hbm), custom_call_target="tpu_custom_call" | custom-call | tf_op jit(solution)/shard_map/transform/pallas_call | solution.py:430
  92.2 0.0 copy-done
  92.2 1.5 %fusion = f32[2,768,128]{1,2,0:T(8,128)S(1)} fusion(bf16[2,768,128]{2,1,0:T(8,128)(2,1)} %bitcast.10, bf16[2,768,768]{2,1,0:T(8,128)(2,1)S(1)} %copy-done, f32[768]{0:T(1024)S(1)} %fusion.4), kind=kOutput, calls=%fused_computation.1 | convolution fusion | flops 302186496 | bytes 3542016 | tf_op jit(solution)/shard_map/kyn,kyc->knc/dot_general | solution.py:497
  93.7 1.1 %copy.9 = f32[2,768,128]{2,1,0:T(8,128)} copy(f32[2,768,128]{1,2,0:T(8,128)S(1)} %fusion) | data formatting | bytes 1572864 | tf_op jit(solution)/shard_map/mul | solution.py:500
  (1 shorter events, 0.0 us)
Async XLA Ops:
  0.0 92.2 %copy-start = (bf16[2,768,768]{2,1,0:T(8,128)(2,1)S(1)}, bf16[2,768,768]{2,1,0:T(8,128)(2,1)}, u32[]{:S(2)}) copy-start(bf16[2,768,768]{2,1,0:T(8,128)(2,1)} %param.12) | copy-start | bytes 7077892

commit v6 on v4

--- a/solution.py
+++ b/solution.py
@@ -136,10 +136,10 @@
 
 def transform_kernel(lon, lat, count_hbm, block_hbm, stencil_hbm, frac_hbm, own_hbm, table_hbm, out_ref, *refs):
     (count_ref, block_ref, stencil_ref, frac_ref, own_ref, small) = refs[:6]
-    (cells_ref, tiles, onehot, weight, departed, sectors, detour, plus, minus, table, total) = refs[6:17]
-    (blocks, landed, bypass, wide, packs, bands) = refs[17:23]
-    (fetch_sem, send_tile, recv_tile, send_row, recv_row, detour_sem, onward_row) = refs[23:30]
-    (send_block, recv_block, bypass_sem, onward_block, send_band, recv_band) = refs[30:]
+    (cells_ref, tiles, onehot, weight, departed, sectors, plus, minus, table, total) = refs[6:16]
+    (blocks, landed, wide, packs, bands) = refs[16:21]
+    (fetch_sem, send_tile, recv_tile, send_row, recv_row) = refs[21:26]
+    (send_block, recv_block, send_band, recv_band) = refs[26:]
     me_lon, me_lat = lax.axis_index("lon"), lax.axis_index("lat")
     rows = departed.shape[0]
     depth = blocks.shape[2]
@@ -148,7 +148,6 @@
     me_chip, me_core = me_lon // 2, me_lon % 2
     tall = 8 if lat == 32 else lat
     flat = lat // tall
-    quarter = (chips // 4, chips - chips // 4)
 
     barrier = pltpu.get_barrier_semaphore()
 
@@ -216,27 +215,6 @@
             device_id_type=MESH,
         )
 
-    def row_detour(row, core):
-        return pltpu.make_async_remote_copy(
-            src_ref=departed.at[row],
-            dst_ref=detour.at[core],
-            send_sem=send_row.at[row],
-            recv_sem=detour_sem.at[core],
-            device_id={"lon": lax.rem(me_chip + quarter[core], chips) * 2 + me_core},
-            device_id_type=MESH,
-        )
-
-    def row_onward(core):
-        source = lax.rem(me_chip + chips - quarter[core], chips) * 2 + me_core
-        return pltpu.make_async_remote_copy(
-            src_ref=detour.at[core],
-            dst_ref=slot_of(source),
-            send_sem=onward_row.at[core],
-            recv_sem=recv_row.at[source],
-            device_id={"lon": lax.rem(me_chip + quarter[core], chips) * 2 + core},
-            device_id_type=MESH,
-        )
-
     parts = rows // CHUNK
 
     def interpolate(part, carry):
@@ -256,15 +234,10 @@
 
         def send_rows(pair, inner):
             chip = part * (CHUNK // 2) + pair
-            opposite = lax.rem(chip + chips - me_chip, chips) == chips // 2
             for core in range(2):
                 row = chip * 2 + core
 
-                @pl.when(opposite)
-                def _():
-                    row_detour(row, core).start()
-
-                @pl.when(jnp.logical_and(jnp.logical_not(opposite), row != me_lon))
+                @pl.when(row != me_lon)
                 def _():
                     row_copy(me_lon, row, row, me_lon).start()
 
@@ -280,9 +253,6 @@
     slot_of(me_lon)[...] = departed[me_lon]
     fill_table(small, plus, minus, table)
     total[...] = jnp.zeros_like(total)
-    for core in range(2):
-        row_detour(0, core).wait_recv()
-        row_onward(core).start()
 
     def accumulate(step, carry):
         chip = lax.rem(me_chip + near_first(step, chips), chips)
@@ -310,32 +280,7 @@
             device_id_type=MESH,
         )
 
-    def block_detour(parity, core):
-        block = lax.rem(me_chip + chips // 2, chips) * 2 + core
-        return pltpu.make_async_remote_copy(
-            src_ref=blocks.at[parity, block],
-            dst_ref=bypass.at[parity, core],
-            send_sem=send_block.at[parity, block],
-            recv_sem=bypass_sem.at[parity, core],
-            device_id={"lon": lax.rem(me_chip + quarter[core], chips) * 2 + me_core},
-            device_id_type=MESH,
-        )
-
-    def block_onward(parity, core):
-        source = lax.rem(me_chip + chips - quarter[core], chips) * 2 + me_core
-        return pltpu.make_async_remote_copy(
-            src_ref=bypass.at[parity, core],
-            dst_ref=landed.at[parity, source],
-            send_sem=onward_block.at[parity, core],
-            recv_sem=recv_block.at[parity, source],
-            device_id={"lon": lax.rem(me_chip + quarter[core], chips) * 2 + core},
-            device_id_type=MESH,
-        )
-
     blocks[...] = total[...].astype(jnp.bfloat16).reshape(blocks.shape)
-    for parity in range(2):
-        for core in range(2):
-            block_detour(parity, core).start()
     for parity in range(2):
 
         def send_blocks(step, carry):
@@ -349,12 +294,7 @@
 
             return carry
 
-        lax.fori_loop(1, chips, send_blocks, 0)
-    for parity in range(2):
-        for core in range(2):
-            block_detour(parity, core).wait_recv()
-            block_onward(parity, core).start()
-
+        lax.fori_loop(0, chips, send_blocks, 0)
     def band_copy(parity, source, target, slot_send, slot_recv):
         return pltpu.make_async_remote_copy(
             src_ref=packs.at[parity, target],
@@ -400,7 +340,6 @@
 
     for side in range(2):
         tile_copy(side).wait_send()
-        row_onward(side).wait_send()
 
     def finish_rows(step, carry):
         peer = lax.rem(me_lon + step, lon)
@@ -410,9 +349,6 @@
         return carry
 
     lax.fori_loop(1, lon, finish_rows, 0)
-    for parity in range(2):
-        for core in range(2):
-            block_onward(parity, core).wait_send()
 
     def finish_bands(step, carry):
         peer = lax.rem(me_lat + step, lat)
@@ -447,14 +383,12 @@
             pltpu.VMEM((COLS, 128), jnp.float32),
             pltpu.VMEM((COLS // 128, 128, 128), jnp.bfloat16),
             pltpu.VMEM((lon // 2, 256, 128), jnp.bfloat16),
-            pltpu.VMEM((2, 128, 128), jnp.bfloat16),
             pltpu.VMEM((FINE, NLON), jnp.float32),
             pltpu.VMEM((FINE, NLON), jnp.float32),
             pltpu.VMEM((NLON // 256, KF, 256), jnp.bfloat16),
             pltpu.VMEM((KF, 128), jnp.float32),
             pltpu.VMEM((2, lon, depth, 128), jnp.bfloat16),
             pltpu.VMEM((2, lon, depth, 128), jnp.bfloat16),
-            pltpu.VMEM((2, 2, depth, 128), jnp.bfloat16),
             pltpu.VMEM((2, lon * depth, 128), jnp.float32),
             pltpu.VMEM(band, jnp.bfloat16),
             pltpu.VMEM(band, jnp.bfloat16),
@@ -463,12 +397,8 @@
             pltpu.SemaphoreType.DMA((2,)),
             pltpu.SemaphoreType.DMA((lon,)),
             pltpu.SemaphoreType.DMA((lon,)),
-            pltpu.SemaphoreType.DMA((2,)),
-            pltpu.SemaphoreType.DMA((2,)),
             pltpu.SemaphoreType.DMA((2, lon)),
             pltpu.SemaphoreType.DMA((2, lon)),
-            pltpu.SemaphoreType.DMA((2, 2)),
-            pltpu.SemaphoreType.DMA((2, 2)),
             pltpu.SemaphoreType.DMA((2, lat)),
             pltpu.SemaphoreType.DMA((2, lat)),
         ],

time: 92.2 us -> 94.3 us (1.023)
  the two profiles are of different devices: /device:TPU:8 before, /device:TPU:1 now
where the time goes in v6:
time: 94.3 us; the launch traced here: 94.1 us
  Pallas kernels  91.4 us (97%)
  matrix products  1.52 us (2%)
  local copies, waits for them, and re-layouts  1.15 us (1%)
    pallas_call x1, Pallas kernels, transform(): pl.pallas_call(functools.partial(transform_kernel, lon, lat), out_shape=j...  91.4 us

profile of v6, /device:TPU:1, one launch (start us, length us, event | category | flops | bytes accessed | tf_op | source)
XLA Modules:
  0.0 94.1 jit_solution(9080343003455839579)
XLA Ops:
  0.0 0.0 copy-start
  0.0 91.4 %transform.1 = bf16[2,32,24,128]{3,2,1,0:T(8,128)(2,1)} custom-call(s32[3]{0:T(128)} %bitcast.15, s32[3,1,1280]{2,1,0:T(1,128)} %bitcast.14, s32[3,4,1280]{2,1,0:T(4,128)} %bitcast.12, s32[3,2,1280]{2,1,0:T(2,128)} %bitcast.13, bf16[3072,128]{1,0:T(8,128)(2,1)} %bitcast.11, f32[416,128]{1,0:T(8,128)} %constant.9.clone.table_hbm), custom_call_target="tpu_custom_call" | custom-call | tf_op jit(solution)/shard_map/transform/pallas_call | solution.py:368
  91.4 0.0 copy-done
  91.4 1.5 %fusion = f32[2,768,128]{1,2,0:T(8,128)S(1)} fusion(bf16[2,768,128]{2,1,0:T(8,128)(2,1)} %bitcast.10, bf16[2,768,768]{2,1,0:T(8,128)(2,1)S(1)} %copy-done, f32[768]{0:T(1024)S(1)} %fusion.4), kind=kOutput, calls=%fused_computation.1 | convolution fusion | flops 302186496 | bytes 3542016 | tf_op jit(solution)/shard_map/kyn,kyc->knc/dot_general | solution.py:426
  93.0 1.1 %copy.9 = f32[2,768,128]{2,1,0:T(8,128)} copy(f32[2,768,128]{1,2,0:T(8,128)S(1)} %fusion) | data formatting | bytes 1572864 | tf_op jit(solution)/shard_map/mul | solution.py:429
  (1 shorter events, 0.0 us)
Async XLA Ops:
  0.0 91.4 %copy-start = (bf16[2,768,768]{2,1,0:T(8,128)(2,1)S(1)}, bf16[2,768,768]{2,1,0:T(8,128)(2,1)}, u32[]{:S(2)}) copy-start(bf16[2,768,768]{2,1,0:T(8,128)(2,1)} %param.12) | copy-start | bytes 7077892
